TPU v7x, 32 devices: a whole 2x2x4 slice. The times are simulated.
32 devices in a mesh: wide: 8 (over z, x), narrow: 4 (over y, core).
Axes of the slice: x: 2, y: 2, z: 4, core: 2. Of those that a mesh axis runs over, the one named last changes fastest.
Arguments:
- stream_one: bfloat16 [12288, 1024], P(('wide', 'narrow')), may hold values from -6 to 6
- stream_two: bfloat16 [12288, 1024], P(('wide', 'narrow')), may hold values from -6 to 6
- attention_gain: float32 [1024], replicated, may hold values from 0.5 to 1.5
- attention_shift: float32 [1024], replicated, may hold values from -1.8 to 1.8
- query_proj: bfloat16 [1024, 1024], P(None, 'narrow'), may hold values from -3.59375 to 3.59375
- value_proj: bfloat16 [1024, 1024], P(None, 'narrow'), may hold values from -0.1875 to 0.1875
- output_proj: bfloat16 [1024, 1024], P('narrow'), may hold values from -0.375 to 0.375
- forward_gain: float32 [1024], replicated, may hold values from 0.5 to 1.5
- forward_shift: float32 [1024], replicated, may hold values from -1.8 to 1.8
- up_proj: bfloat16 [1024, 4096], P(None, 'narrow'), may hold values from -0.1875 to 0.1875
- up_bias: float32 [4096], P('narrow'), may hold values from -1.8 to 1.8
- down_proj: bfloat16 [4096, 1024], P('narrow'), may hold values from -0.125 to 0.125
- down_bias: float32 [1024], replicated, may hold values from -1.8 to 1.8
- bucket_ids: int32 [12288, 4], P(('wide', 'narrow')), may hold values from 0 to 23
- sort_orders: int32 [8, 4, 1536], P('wide'), may hold values from 0 to 1535, as said below
- doc_lengths: int32 [8, 8], P('wide'), may hold values from 1 to 768, 1536 in all within a row
- cotan_one: bfloat16 [12288, 1024], P(('wide', 'narrow'))
- cotan_two: bfloat16 [12288, 1024], P(('wide', 'narrow'))
Outputs:
- output_one: bfloat16 [12288, 1024], P(('wide', 'narrow'))
- output_two: bfloat16 [12288, 1024], P(('wide', 'narrow'))
- grad_one: bfloat16 [12288, 1024], P(('wide', 'narrow'))
- grad_two: bfloat16 [12288, 1024], P(('wide', 'narrow'))
- grad_attention_gain: float32 [1024], replicated
- grad_attention_shift: float32 [1024], replicated
- grad_query_proj: float32 [1024, 1024], P(None, 'narrow')
- grad_value_proj: float32 [1024, 1024], P(None, 'narrow')
- grad_output_proj: float32 [1024, 1024], P('narrow')
- grad_forward_gain: float32 [1024], replicated
- grad_forward_shift: float32 [1024], replicated
- grad_up_proj: float32 [1024, 4096], P(None, 'narrow')
- grad_up_bias: float32 [4096], P('narrow')
- grad_down_proj: float32 [4096, 1024], P('narrow')
- grad_down_bias: float32 [1024], replicated
- bucket_counts: int32 [4, 24], replicated
Inputs may be any that keep to these rules, and one draw needn't show every extreme that they name: sort_orders[s, r] lists the 1536 positions of sequence s by increasing bucket of round r, ties by position. `doc_lengths`: the 8 documents of a sequence fill its 1536 positions in order.
All inputs are finite; a program needn't handle non-finite values.
Results may differ from a plain program's by a relative error of at most 0.019.
Values may be sent and summed in bfloat16 or wider, within the bound.
A program may use at most 256 MiB of HBM per device.

v0:
```python
from functools import partial
import math

import jax
import jax.numpy as jnp
from jax import lax
from jax.sharding import PartitionSpec as P

HD = 128
GROUP = 64
NB = 24


FLOAT = jnp.float32
HALF = jnp.bfloat16


def normalize(inputs):
    center = inputs - jnp.mean(inputs, axis=-1, keepdims=True)
    inverse = lax.rsqrt(jnp.mean(center * center, axis=-1, keepdims=True) + 1e-05)
    return (center * inverse, inverse)


def norm_back(grad_out, scaled, inverse, gain):
    spread = grad_out * gain
    return inverse * (
        spread
        - jnp.mean(spread, axis=-1, keepdims=True)
        - scaled * jnp.mean(spread * scaled, axis=-1, keepdims=True)
    )


def window_of(blocks):
    return jnp.concatenate([jnp.roll(blocks, 1, axis=1), blocks], axis=2)


def fold_window(window):
    return window[:, :, GROUP:] + jnp.roll(window[:, :, :GROUP], -1, axis=1)


def contract_rows(left, right):
    return lax.dot_general(left, right, (((0,), (0,)), ((), ())), preferred_element_type=FLOAT)


def times_transpose(left, right):
    return lax.dot_general(left, right, (((1,), (1,)), ((), ())), preferred_element_type=FLOAT)


def invert(ordering):
    total_len = ordering.shape[0]
    return (
        jnp.zeros((total_len,), jnp.int32).at[ordering].set(jnp.arange(total_len, dtype=jnp.int32))
    )


def pick_rows(matrix, indices):
    return jnp.take(matrix, indices, axis=0)


def by_round(table, indices):
    return jax.vmap(pick_rows)(table, indices)


def per_device(
    stream_one,
    stream_two,
    attention_gain,
    attention_shift,
    query_proj,
    value_proj,
    output_proj,
    forward_gain,
    forward_shift,
    up_proj,
    up_bias,
    down_proj,
    down_bias,
    bucket_ids,
    sort_orders,
    doc_lengths,
    cotan_one,
    cotan_two,
):
    local_rows = stream_one.shape[0]
    first_rows = stream_one.astype(FLOAT)
    second_rows = stream_two.astype(FLOAT)
    orderings = sort_orders[0]
    round_count = orderings.shape[0]
    length = orderings.shape[1]
    blocks = length // GROUP
    head_count = query_proj.shape[1] // HD
    factor = 1.0 / math.sqrt(HD)
    places = jnp.arange(length, dtype=jnp.int32)
    doc_ends = jnp.cumsum(doc_lengths[0])
    segment = jnp.sum(
        (places[:, None] >= doc_ends[None, :]).astype(jnp.int32), axis=-1, dtype=jnp.int32
    )
    inverse = jax.vmap(invert)(orderings)
    pos_rows = orderings.reshape(round_count, blocks, GROUP)
    seg_rows = jnp.take(segment, orderings, axis=0).reshape(round_count, blocks, GROUP)
    pos_window = window_of(pos_rows)
    seg_window = window_of(seg_rows)
    allowed = (seg_window[:, :, None, :] == seg_rows[..., None]) & (
        pos_window[:, :, None, :] <= pos_rows[..., None]
    )
    itself = pos_window[:, :, None, :] == pos_rows[..., None]
    scaled_one, inverse_one = normalize(second_rows)
    normed_one = (scaled_one * attention_gain + attention_shift).astype(HALF)
    gathered_one = lax.all_gather(normed_one, "narrow", axis=0, tiled=True)
    queries = (
        jnp.dot(gathered_one, query_proj, preferred_element_type=FLOAT)
        .astype(HALF)
        .reshape(length, head_count, HD)
    )
    query_float = queries.astype(FLOAT)
    key_scale = lax.rsqrt(jnp.sum(query_float * query_float, axis=-1, keepdims=True) + 1e-06)
    unit_keys = query_float * key_scale
    key_low = unit_keys.astype(HALF)
    value_rows = (
        jnp.dot(gathered_one, value_proj, preferred_element_type=FLOAT)
        .astype(HALF)
        .reshape(length, head_count, HD)
    )
    sorted_shape = (round_count, blocks, GROUP, head_count, HD)
    query_sorted = jnp.take(queries, orderings, axis=0).reshape(sorted_shape)
    key_window = window_of(jnp.take(key_low, orderings, axis=0).reshape(sorted_shape))
    value_window = window_of(jnp.take(value_rows, orderings, axis=0).reshape(sorted_shape))

    def masked_scores():
        raw_scores = (
            jnp.einsum("rcihd,rcjhd->rchij", query_sorted, key_window, preferred_element_type=FLOAT)
            * factor
        )
        raw_scores = jnp.where(itself[:, :, None], -100000.0, raw_scores)
        return jnp.where(allowed[:, :, None], raw_scores, -1000000000.0)

    scores = masked_scores()
    row_max = jnp.max(scores, axis=-1, keepdims=True)
    row_total = jnp.sum(jnp.exp(scores - row_max), axis=-1, keepdims=True)
    log_total = row_max + jnp.log(row_total)
    probs_low = (jnp.exp(scores - row_max) / row_total).astype(HALF)
    mixture = jnp.einsum(
        "rchij,rcjhd->rcihd", probs_low, value_window, preferred_element_type=FLOAT
    )
    round_outs = by_round(mixture.reshape(round_count, length, head_count, HD), inverse)
    sorted_sums = jnp.swapaxes(log_total[..., 0], 2, 3).reshape(round_count, length, head_count)
    round_sums = by_round(sorted_sums, inverse)
    round_peak = jnp.max(round_sums, axis=0, keepdims=True)
    shares = jnp.exp(round_sums - round_peak)
    shares = shares / jnp.sum(shares, axis=0, keepdims=True)
    merged = (
        jnp.sum(shares[..., None] * round_outs, axis=0)
        .reshape(length, head_count * HD)
        .astype(HALF)
    )
    attended = lax.psum_scatter(
        jnp.dot(merged, output_proj, preferred_element_type=FLOAT),
        "narrow",
        scatter_dimension=0,
        tiled=True,
    )
    middle = first_rows + attended
    scaled_two, inverse_two = normalize(middle)
    normed_two = (scaled_two * forward_gain + forward_shift).astype(HALF)
    gathered_two = lax.all_gather(normed_two, "narrow", axis=0, tiled=True)
    hidden = jnp.dot(gathered_two, up_proj, preferred_element_type=FLOAT) + up_bias
    active_float, gelu_back = jax.vjp(partial(jax.nn.gelu, approximate=True), hidden)
    active = active_float.astype(HALF)
    fed_rows = lax.psum_scatter(
        jnp.dot(
            lax.slice_in_dim(active, 0, lax.axis_size("narrow") * local_rows, axis=0),
            down_proj,
            preferred_element_type=FLOAT,
        ).astype(jnp.bfloat16),
        "narrow",
        scatter_dimension=0,
        tiled=True,
    ).astype(jnp.float32)
    result_two = second_rows + (fed_rows + down_bias)
    grad_out_two = lax.all_gather(cotan_two, "narrow", axis=0, tiled=True)
    grad_down = contract_rows(active, grad_out_two)
    grad_down_bias = jnp.sum(grad_out_two, axis=0, dtype=FLOAT)
    grad_hidden = gelu_back(times_transpose(grad_out_two, down_proj))[0].astype(HALF)
    grad_up = contract_rows(gathered_two, grad_hidden)
    grad_up_bias = jnp.sum(grad_hidden, axis=0, dtype=FLOAT)
    grad_normed_two = lax.psum_scatter(
        times_transpose(grad_hidden, up_proj).astype(jnp.bfloat16),
        "narrow",
        scatter_dimension=0,
        tiled=True,
    ).astype(jnp.float32)
    grad_middle = cotan_one.astype(FLOAT) + norm_back(
        grad_normed_two, scaled_two, inverse_two, forward_gain
    )
    grad_first_low = grad_middle.astype(HALF)
    grad_rows = lax.all_gather(grad_first_low, "narrow", axis=0, tiled=True)
    grad_output = contract_rows(merged, grad_rows)
    grad_merged = (
        times_transpose(grad_rows, output_proj)
        .astype(HALF)
        .astype(FLOAT)
        .reshape(length, head_count, HD)
    )
    grad_shares = jnp.sum(round_outs * grad_merged, axis=-1)
    grad_logs = shares * (grad_shares - jnp.sum(shares * grad_shares, axis=0, keepdims=True))
    grad_round = (shares[..., None] * grad_merged).astype(HALF)
    grad_mix = by_round(grad_round, orderings).reshape(sorted_shape)
    grad_log_sorted = jnp.swapaxes(
        by_round(grad_logs, orderings).reshape(round_count, blocks, GROUP, head_count), 2, 3
    )
    scores_again = masked_scores()
    probabilities = jnp.exp(scores_again - row_max) / row_total
    grad_probs = jnp.einsum(
        "rcihd,rcjhd->rchij", grad_mix, value_window, preferred_element_type=FLOAT
    )
    grad_scores = probabilities * (
        grad_probs
        - jnp.sum(probabilities * grad_probs, axis=-1, keepdims=True)
        + grad_log_sorted[..., None]
    )
    grad_scores = jnp.where(itself[:, :, None], 0.0, grad_scores).astype(HALF)
    grad_query_sorted = (
        jnp.einsum("rchij,rcjhd->rcihd", grad_scores, key_window, preferred_element_type=FLOAT)
        * factor
    )
    grad_key_window = (
        jnp.einsum("rchij,rcihd->rcjhd", grad_scores, query_sorted, preferred_element_type=FLOAT)
        * factor
    )
    grad_value_window = jnp.einsum(
        "rchij,rcihd->rcjhd", probabilities.astype(HALF), grad_mix, preferred_element_type=FLOAT
    )

    def restore(sorted_grad):
        return jnp.sum(
            by_round(sorted_grad.reshape(round_count, length, head_count, HD), inverse), axis=0
        )

    grad_query = restore(grad_query_sorted)
    grad_key = restore(fold_window(grad_key_window))
    grad_value = (
        restore(fold_window(grad_value_window)).reshape(length, head_count * HD).astype(HALF)
    )
    key_along = jnp.sum(grad_key * unit_keys, axis=-1, keepdims=True)
    grad_query_total = (
        (grad_query + key_scale * (grad_key - unit_keys * key_along))
        .reshape(length, head_count * HD)
        .astype(HALF)
    )
    grad_query_weights = contract_rows(gathered_one, grad_query_total)
    grad_value_weights = contract_rows(gathered_one, grad_value)
    grad_normed_one = lax.psum_scatter(
        (
            times_transpose(grad_query_total, query_proj) + times_transpose(grad_value, value_proj)
        ).astype(jnp.bfloat16),
        "narrow",
        scatter_dimension=0,
        tiled=True,
    ).astype(jnp.float32)
    grad_second = cotan_two.astype(FLOAT) + norm_back(
        grad_normed_one, scaled_one, inverse_one, attention_gain
    )
    levels = jnp.arange(NB, dtype=jnp.int32)
    counts = jnp.sum((bucket_ids[:, :, None] == levels).astype(FLOAT), axis=0)
    norm_totals = lax.psum(
        (
            jnp.sum(grad_normed_one * scaled_one, axis=0),
            jnp.sum(grad_normed_one, axis=0),
            jnp.sum(grad_normed_two * scaled_two, axis=0),
            jnp.sum(grad_normed_two, axis=0),
            counts,
        ),
        ("wide", "narrow"),
    )
    together = lax.psum(
        (
            grad_query_weights,
            grad_value_weights,
            grad_output,
            grad_up,
            grad_up_bias,
            grad_down,
            grad_down_bias,
        ),
        "wide",
    )
    attention_sums = together[:3]
    forward_sums = together[3:]
    return (
        middle.astype(HALF),
        result_two.astype(HALF),
        grad_first_low,
        grad_second.astype(HALF),
        norm_totals[0],
        norm_totals[1],
        attention_sums[0],
        attention_sums[1],
        attention_sums[2],
        norm_totals[2],
        norm_totals[3],
        forward_sums[0],
        forward_sums[1],
        forward_sums[2],
        forward_sums[3],
        norm_totals[4].astype(jnp.int32),
    )


def solution(mesh):
    return jax.shard_map(
        per_device,
        mesh=mesh,
        in_specs=(
            P(("wide", "narrow"), None),
            P(("wide", "narrow"), None),
            P(),
            P(),
            P(None, "narrow"),
            P(None, "narrow"),
            P("narrow", None),
            P(),
            P(),
            P(None, "narrow"),
            P("narrow"),
            P("narrow", None),
            P(),
            P(("wide", "narrow"), None),
            P("wide", None, None),
            P("wide", None),
            P(("wide", "narrow"), None),
            P(("wide", "narrow"), None),
        ),
        out_specs=(
            P(("wide", "narrow"), None),
            P(("wide", "narrow"), None),
            P(("wide", "narrow"), None),
            P(("wide", "narrow"), None),
            P(),
            P(),
            P(None, "narrow"),
            P(None, "narrow"),
            P("narrow", None),
            P(),
            P(),
            P(None, "narrow"),
            P("narrow"),
            P("narrow", None),
            P(),
            P(),
        ),
        check_vma=False,
    )
```

profile of v0, /device:TPU:0, one launch (start us, length us, event | category | flops | bytes accessed | tf_op | source)
XLA Modules:
  0.0 1809.7 jit_solution(14061170866485726974)
XLA Ops:
  13.4 23.2 %scatter_custom_fusion = s32[6144]{0:T(1024)S(1)} fusion(s32[6144]{0:T(1024)S(1)} %reshape.342, s32[6144]{0:T(1024)S(1)} %reshape.344, s32[]{:T(128)} %constant.48.clone.1), kind=kCustom, calls=%fused_computation.167 | custom fusion | bytes 24580
  36.8 34.3 %gather_fusion = s32[6144]{0:T(1024)S(1)} fusion(s32[1536]{0:T(1024)S(1)} %convert_reduce_fusion.6, s32[6144]{0:T(1024)S(1)} %broadcast_clamp_fusion.1), kind=kCustom, calls=%fused_computation.9 | custom fusion | bytes 73728 | tf_op jit(solution)/shard_map/jit(_take)/gather | solution.py:100
  93.0 40.3 %gather_fusion.2 = bf16[6144,2,128]{2,1,0:T(2,128)(2,1)} fusion(bf16[1536,2,128]{2,1,0:T(2,128)(2,1)S(1)} %copy.131, s32[6144]{0:T(1024)S(1)} %broadcast_clamp_fusion), kind=kCustom, calls=%fused_computation.clone | custom fusion | bytes 6316032 | tf_op jit(solution)/shard_map/jit(_take)/gather | solution.py:125
  133.3 41.9 %gather_fusion.5 = bf16[6144,2,128]{2,1,0:T(2,128)(2,1)} fusion(bf16[1536,2,128]{2,1,0:T(2,128)(2,1)} %copy.140, s32[6144]{0:T(1024)S(1)} %broadcast_clamp_fusion), kind=kCustom, calls=%fused_computation.4.clone | custom fusion | bytes 6316032 | tf_op jit(solution)/shard_map/jit(_take)/gather | solution.py:127
  175.3 40.8 %gather_fusion.3 = bf16[6144,2,128]{2,1,0:T(2,128)(2,1)} fusion(bf16[1536,2,128]{2,1,0:T(2,128)(2,1)S(1)} %copy-done.9, s32[6144]{0:T(1024)S(1)} %broadcast_clamp_fusion), kind=kCustom, calls=%fused_computation.3.clone | custom fusion | bytes 6316032 | tf_op jit(solution)/shard_map/jit(_take)/gather | solution.py:126
  239.5 93.9 %gather_fusion.4 = f32[6144,2]{1,0:T(8,128)} fusion(f32[4,1536,2]{2,1,0:T(8,128)} %bitcast.123, s32[6144]{0:T(1024)S(1)} %reshape.396), kind=kCustom, calls=%fused_computation.1.clone | custom fusion | bytes 147456 | tf_op jit(solution)/shard_map/vmap(jit(_take))/gather | solution.py:57
  351.4 18.1 copy.146
  369.5 55.0 %gather_fusion.6 = f32[6144,2,128]{2,1,0:T(2,128)} fusion(f32[4,1536,2,128]{3,2,1,0:T(2,128)} %copy.146, s32[6144]{0:T(1024)S(1)} %reshape.396), kind=kCustom, calls=%fused_computation.2.clone | custom fusion | bytes 12632064 | tf_op jit(solution)/shard_map/vmap(jit(_take))/gather | solution.py:57
  424.5 18.4 %multiply_reduce_fusion.2 = bf16[1536,2,128]{2,1,0:T(2,128)(2,1)S(1)} fusion(f32[4,1536,2,128]{3,2,1,0:T(2,128)} %bitcast.129, pred[4,1536]{1,0:T(4,128)(4,1)S(1)} %compare_and_fusion.2, f32[4,1536,2]{2,1,0:T(8,128)} %fusion.29), kind=kLoop, calls=%fused_computation.40 | loop fusion | flops 4325376 | bytes 7133184 | tf_op jit(solution)/shard_map/reduce_sum | solution.py:152
  447.6 61.1 %reduce-scatter.5.cloned.1.call-done = f32[384,1024]{1,0:T(8,128)} async-done(((f32[1536,1024]{1,0:T(8,128)}), f32[384,1024]{1,0:T(8,128)}) %reduce-scatter.5.cloned.1.call-update) | async-done | bytes 1572880 | tf_op jit(solution)/shard_map/reduce_scatter | solution.py:156
  514.0 27.7 %all-gather.7.cloned.1.call-done = bf16[1536,1024]{1,0:T(8,128)(2,1)} async-done(((bf16[384,1024]{1,0:T(8,128)(2,1)}), bf16[1536,1024]{1,0:T(8,128)(2,1)}) %all-gather.7.cloned.1.call-update) | async-done | bytes 3145744 | tf_op jit(solution)/shard_map/all_gather | solution.py:165
  550.2 21.5 %all-gather.9.cloned.1.call-done = bf16[1536,1024]{1,0:T(8,128)(2,1)} async-done(((bf16[384,1024]{1,0:T(8,128)(2,1)}), bf16[1536,1024]{1,0:T(8,128)(2,1)}) %all-gather.9.cloned.1.call-update) | async-done | bytes 3145744 | tf_op jit(solution)/shard_map/all_gather | solution.py:180
  571.7 11.4 convert_reduce_fusion.1
  589.8 38.1 %reduce-scatter.9.cloned.1.call-done = bf16[384,1024]{1,0:T(8,128)(2,1)} async-done(((bf16[1536,1024]{1,0:T(8,128)(2,1)}), bf16[384,1024]{1,0:T(8,128)(2,1)}) %reduce-scatter.9.cloned.1.call-update) | async-done | bytes 786448 | tf_op jit(solution)/shard_map/reduce_scatter | solution.py:186
  636.2 26.6 %all-gather.11.cloned.1.call-done = bf16[1536,1024]{1,0:T(8,128)(2,1)} async-done(((bf16[384,1024]{1,0:T(8,128)(2,1)}), bf16[1536,1024]{1,0:T(8,128)(2,1)}) %all-gather.11.cloned.1.call-update) | async-done | bytes 3145744 | tf_op jit(solution)/shard_map/all_gather | solution.py:196
  669.9 10.1 multiply_convert_fusion
  680.0 50.0 %gather_fusion.1 = bf16[6144,2,128]{2,1,0:T(2,128)(2,1)} fusion(bf16[4,1536,2,128]{3,2,1,0:T(2,128)(2,1)} %multiply_convert_fusion, s32[6144]{0:T(1024)S(1)} %reshape.336), kind=kCustom, calls=%fused_computation.10 | custom fusion | bytes 6340608 | tf_op jit(solution)/shard_map/vmap(jit(_take))/gather | solution.py:57
  740.9 13.2 convolution_bitcast_fusion
  764.2 18.1 copy.163
  782.2 55.0 %gather_fusion.10 = f32[6144,2,128]{2,1,0:T(2,128)} fusion(f32[4,1536,2,128]{3,2,1,0:T(2,128)} %copy.163, s32[6144]{0:T(1024)S(1)} %reshape.396), kind=kCustom, calls=%fused_computation.8.clone | custom fusion | bytes 12632064 | tf_op jit(solution)/shard_map/vmap(jit(_take))/gather | solution.py:57
  837.3 22.2 %select_reduce_fusion = (bf16[1536,2,128]{2,1,0:T(2,128)(2,1)}, f32[4,1536,2]{2,1,0:T(8,128)}) fusion(f32[4,1536,2,128]{3,2,1,0:T(2,128)} %bitcast.137, pred[4,1536]{1,0:T(4,128)(4,1)S(1)} %compare_and_fusion.2, f32[1536,2,128]{2,1,0:T(2,128)} %copy.147, f32[4,1536,2,128]{3,2,1,0:T(2,128)} %bitcast.130), kind=kLoop, calls=%fused_computation.27 | loop fusion | flops 7458816 | bytes 14997504 | tf_op jit(solution)/shard_map/reduce_sum | solution.py:235
  867.4 94.3 %gather_fusion.7 = f32[6144,2]{1,0:T(8,128)} fusion(f32[4,1536,2]{2,1,0:T(8,128)} %subtract_multiply_fusion, s32[6144]{0:T(1024)S(1)} %reshape.410), kind=kCustom, calls=%fused_computation.5.clone | custom fusion | bytes 147456 | tf_op jit(solution)/shard_map/vmap(jit(_take))/gather | solution.py:57
  964.3 91.2 %multiply_bitcast_fusion.1 = f32[4,24,64,2,128]{4,2,3,1,0:T(8,128)} fusion(bf16[4,23,64,2,128]{4,2,3,1,0:T(8,128)(2,1)} %copy-done.35, bf16[4,1,64,2,128]{4,2,3,1,0:T(8,128)(2,1)S(1)} %copy-done.48, f32[4,24,2,64,128]{4,3,2,1,0:T(8,128)} %fusion.24, f32[4,24,2,64]{3,2,1,0:T(2,128)S(1)} %copy.151, pred[4,24,64,128]{3,2,1,0:T(8,128)(4,1)} %get-tuple-element.54, ...), kind=kOutput, calls=%fused_computation.33 | convolution fusion | flops 448278656 | bytes 26886144 | tf_op jit(solution)/shard_map/rchij,rcjhd->rcihd/dot_general | solution.py:223
  1055.5 95.0 %multiply_bitcast_fusion = f32[4,24,128,2,128]{4,2,3,1,0:T(8,128)} fusion(f32[4,24,2,64,128]{4,3,2,1,0:T(8,128)} %fusion.24, f32[4,24,2,64]{3,2,1,0:T(2,128)S(1)} %copy.151, pred[4,24,64,128]{3,2,1,0:T(8,128)(4,1)} %get-tuple-element.54, bf16[4,24,64,2,128]{4,2,1,3,0:T(8,128)(2,1)} %bitcast.160, f32[4,24,2,64,128]{4,3,2,1,0:T(8,128)} %copy-done.18, ...), kind=kOutput, calls=%fused_computation.13 | convolution fusion | flops 430977152 | bytes 30031872 | tf_op jit(solution)/shard_map/rchij,rcihd->rcjhd/dot_general | solution.py:227
  1159.4 18.1 copy.153
  1177.5 55.2 %gather_fusion.8 = f32[6144,2,128]{2,1,0:T(2,128)} fusion(f32[4,1536,2,128]{3,2,1,0:T(2,128)} %copy.153, s32[6144]{0:T(1024)S(1)} %reshape.396), kind=kCustom, calls=%fused_computation.6.clone | custom fusion | bytes 12632064 | tf_op jit(solution)/shard_map/vmap(jit(_take))/gather | solution.py:57
  1239.3 18.1 copy.158
  1257.3 55.0 %gather_fusion.9 = f32[6144,2,128]{2,1,0:T(2,128)} fusion(f32[4,1536,2,128]{3,2,1,0:T(2,128)} %copy.158, s32[6144]{0:T(1024)S(1)} %reshape.396), kind=kCustom, calls=%fused_computation.7.clone | custom fusion | bytes 12632064 | tf_op jit(solution)/shard_map/vmap(jit(_take))/gather | solution.py:57
  1312.4 13.8 select_reduce_fusion.2
  1384.6 22.3 %all-reduce.1 = (f32[1024]{0:T(1024)}, f32[1024]{0:T(1024)}) all-reduce(f32[1024]{0:T(1024)S(1)} %copy-done.65, f32[1024]{0:T(1024)S(1)} %convert_reduce_fusion), channel_id=1, replica_groups=mesh['wide'=8,'narrow'=4] {'wide'}, use_global_device_ids=true, to_apply=%region_41.45 | all-reduce | flops 2048 | bytes 16384 | tf_op jit(solution)/shard_map/psum | solution.py:275
  1408.9 37.6 %all-reduce = (f32[1024]{0:T(1024)}, f32[1024]{0:T(1024)}, f32[1024]{0:T(1024)}, f32[1024]{0:T(1024)}, f32[4,24]{1,0:T(4,128)S(1)}) all-reduce(f32[1024]{0:T(1024)S(1)} %get-tuple-element.21, f32[1024]{0:T(1024)S(1)} %get-tuple-element.26, f32[1024]{0:T(1024)S(1)} %copy-done.60, ...), channel_id=1, replica_groups=mesh['wide'=8,'narrow'=4] {'wide','narrow'}, use_global_device_ids=true, to_apply=%region_29.33 | all-reduce | flops 4192 | bytes 33536 | tf_op jit(solution)/shard_map/psum | solution.py:265
  1450.6 341.0 %all-reduce.5.cloned.1.call-done = (f32[1024,256]{1,0:T(8,128)}, f32[1024,256]{1,0:T(8,128)}, f32[256,1024]{1,0:T(8,128)}, f32[1024,1024]{1,0:T(8,128)}, f32[1024,1024]{1,0:T(8,128)}) async-done(((f32[1024,256]{1,0:T(8,128)}, f32[1024,256]{1,0:T(8,128)}, f32[256,1024]{1,0:T(8,128)}, f32[1024,1024]{1,0:T(8,128)}, f32[1024,1024]{1,0:T(8,128)}), (f32[1024,256]{1,0:T(8,128)}, f32[1024,256]{1,0:T(8,128)}, ...) | async-done | bytes 11534352 | tf_op jit(solution)/shard_map/psum | solution.py:275
  (299 shorter events, 232.2 us)
Async XLA Ops:
  7.2 564.5 %copy-start = (bf16[1024,1024]{1,0:T(8,128)(2,1)S(1)}, bf16[1024,1024]{1,0:T(8,128)(2,1)}, u32[]{:S(2)}) copy-start(bf16[1024,1024]{1,0:T(8,128)(2,1)} %param.35) | copy-start | bytes 6291460
  7.2 68.3 %all-gather.5.cloned.1.call-start = ((), (), s32[]{:S(2)}) async-start(), calls=%async_computation.4 | async-start | bytes 3932160 | tf_op jit(solution)/shard_map/all_gather | solution.py:109
  12.7 496.0 %reduce-scatter.5.cloned.1.call-start = ((), (), s32[]{:S(2)}) async-start(), calls=%async_computation.5 | async-start | bytes 7864320 | tf_op jit(solution)/shard_map/reduce_scatter | solution.py:156
  36.8 38.8 %copy-start.38 = (bf16[1024,256]{1,0:T(8,128)(2,1)S(1)}, bf16[1024,256]{1,0:T(8,128)(2,1)}, u32[]{:S(2)}) copy-start(bf16[1024,256]{1,0:T(8,128)(2,1)} %param.28) | copy-start | bytes 1572868
  75.5 140.6 %copy-start.51 = (pred[4,1536]{1,0:T(4,128)(4,1)}, pred[4,1536]{1,0:T(4,128)(4,1)S(1)}, u32[]{:S(2)}) copy-start(pred[4,1536]{1,0:T(4,128)(4,1)S(1)} %compare_and_fusion.3) | copy-start | bytes 18436
  81.6 11.5 copy-start.3
  133.3 41.9 %copy-start.9 = (bf16[1536,2,128]{2,1,0:T(2,128)(2,1)S(1)}, bf16[1536,2,128]{2,1,0:T(2,128)(2,1)}, u32[]{:S(2)}) copy-start(bf16[1536,2,128]{2,1,0:T(2,128)(2,1)} %fusion.44) | copy-start | bytes 2359300
  224.0 117.6 %copy-start.49 = (bf16[4,1,64,2,128]{4,2,3,1,0:T(8,128)(2,1)}, bf16[4,1,64,2,128]{4,2,3,1,0:T(8,128)(2,1)S(1)}, u32[]{:S(2)}) copy-start(bf16[4,1,64,2,128]{4,2,3,1,0:T(8,128)(2,1)S(1)} %copy.212) | copy-start | bytes 393220
  233.2 108.4 %copy-start.42 = (f32[4,24,2,64]{3,2,1,0:T(2,128)}, f32[4,24,2,64]{3,2,1,0:T(2,128)S(1)}, u32[]{:S(2)}) copy-start(f32[4,24,2,64]{3,2,1,0:T(2,128)S(1)} %get-tuple-element.61) | copy-start | bytes 147460
  237.2 104.4 %copy-start.44 = (f32[4,24,2,64]{3,2,1,0:T(2,128)}, f32[4,24,2,64]{3,2,1,0:T(2,128)S(1)}, u32[]{:S(2)}) copy-start(f32[4,24,2,64]{3,2,1,0:T(2,128)S(1)} %fusion.10) | copy-start | bytes 147460
  424.5 19.3 %copy-start.37 = (bf16[256,1024]{1,0:T(8,128)(2,1)S(1)}, bf16[256,1024]{1,0:T(8,128)(2,1)}, u32[]{:S(2)}) copy-start(bf16[256,1024]{1,0:T(8,128)(2,1)} %param.30) | copy-start | bytes 1572868
  447.5 64.2 %copy-start.57 = (f32[1024]{0:T(1024)S(1)}, f32[1024]{0:T(1024)}, u32[]{:S(2)}) copy-start(f32[1024]{0:T(1024)} %param.31) | copy-start | bytes 12292
  447.5 64.2 %copy-start.63 = (f32[1024]{0:T(1024)S(1)}, f32[1024]{0:T(1024)}, u32[]{:S(2)}) copy-start(f32[1024]{0:T(1024)} %param.32) | copy-start | bytes 12292
  447.5 94.1 %all-gather.7.cloned.1.call-start = ((), (), s32[]{:S(2)}) async-start(), calls=%async_computation.6 | async-start | bytes 3932160 | tf_op jit(solution)/shard_map/all_gather | solution.py:165
  512.9 58.8 %all-gather.9.cloned.1.call-start = ((), (), s32[]{:S(2)}) async-start(), calls=%async_computation.8 | async-start | bytes 3932160 | tf_op jit(solution)/shard_map/all_gather | solution.py:180
  513.5 58.2 %copy-start.72 = (f32[1024]{0:T(1024)S(1)}, f32[1024]{0:T(1024)}, u32[]{:S(2)}) copy-start(f32[1024]{0:T(1024)} %param.34) | copy-start | bytes 12292
  513.5 114.3 %reduce-scatter.9.cloned.1.call-start = ((), (), s32[]{:S(2)}) async-start(), calls=%async_computation.9 | async-start | bytes 3932160 | tf_op jit(solution)/shard_map/reduce_scatter | solution.py:186
  571.7 13.0 copy-start.71
  589.7 73.1 %all-gather.11.cloned.1.call-start = ((), (), s32[]{:S(2)}) async-start(), calls=%async_computation.10 | async-start | bytes 3932160 | tf_op jit(solution)/shard_map/all_gather | solution.py:196
  634.1 772.8 %reduce-scatter.11.cloned.1.call-start = ((), (), s32[]{:S(2)}) async-start(), calls=%async_computation.11 | async-start | bytes 3932160 | tf_op jit(solution)/shard_map/reduce_scatter | solution.py:252
  680.0 52.5 %copy-start.50 = (bf16[4,1,64,2,128]{4,2,3,1,0:T(8,128)(2,1)S(1)}, bf16[4,1,64,2,128]{4,2,3,1,0:T(8,128)(2,1)}, u32[]{:S(2)}) copy-start(bf16[4,1,64,2,128]{4,2,3,1,0:T(8,128)(2,1)} %copy-done.49) | copy-start | bytes 393220
  730.0 10.9 slice-start.2
  1312.4 13.8 copy-start.4
  1347.0 100.1 %reduce-scatter.7.cloned.1.call-start = ((), (), s32[]{:S(2)}) async-start(), calls=%async_computation.7 | async-start | bytes 3932160 | tf_op jit(solution)/shard_map/reduce_scatter | solution.py:169
  1356.4 435.2 %all-reduce.5.cloned.1.call-start = ((), (), s32[]{:S(2)}) async-start(), calls=%async_computation.12 | async-start | bytes 23068672 | tf_op jit(solution)/shard_map/psum | solution.py:275
  1381.9 25.0 %copy-start.8 = (bf16[384,1024]{1,0:T(8,128)(2,1)S(1)}, bf16[384,1024]{1,0:T(8,128)(2,1)}, u32[]{:S(2)}) copy-start(bf16[384,1024]{1,0:T(8,128)(2,1)} %param.25) | copy-start | bytes 2359300
  1381.9 25.0 %copy-start.54 = (f32[384]{0:T(512)S(1)}, f32[384]{0:T(512)}, u32[]{:S(2)}) copy-start(f32[384]{0:T(512)} %copy-done.53) | copy-start | bytes 4612
  1381.9 25.0 %copy-start.56 = (f32[1024]{0:T(1024)S(1)}, f32[1024]{0:T(1024)}, u32[]{:S(2)}) copy-start(f32[1024]{0:T(1024)} %param.26) | copy-start | bytes 12292
  1381.9 25.0 %copy-start.59 = (f32[384]{0:T(512)S(1)}, f32[384]{0:T(512)}, u32[]{:S(2)}) copy-start(f32[384]{0:T(512)} %copy-done.58) | copy-start | bytes 4612
  1381.9 27.0 %copy-start.60 = (f32[1024]{0:T(1024)S(1)}, f32[1024]{0:T(1024)}, u32[]{:S(2)}) copy-start(f32[1024]{0:T(1024)} %get-tuple-element.19) | copy-start | bytes 12292
  1381.9 27.0 %copy-start.61 = (f32[1024]{0:T(1024)S(1)}, f32[1024]{0:T(1024)}, u32[]{:S(2)}) copy-start(f32[1024]{0:T(1024)} %get-tuple-element.25) | copy-start | bytes 12292
  1381.9 65.1 %copy-start.64 = (f32[1024]{0:T(1024)S(1)}, f32[1024]{0:T(1024)}, u32[]{:S(2)}) copy-start(f32[1024]{0:T(1024)} %param.36) | copy-start | bytes 12292
  (57 other events, 239.2 us)
Sparse Core Ops, SparseCore 0:
  12.8 31.2 all-gather.4
  447.6 61.0 reduce-scatter.4
  513.1 28.5 all-gather.6
  543.1 28.5 all-gather.8
  589.8 37.9 reduce-scatter.8
  634.2 28.5 all-gather.10
  1347.1 37.9 reduce-scatter.10
  1387.8 38.6 reduce-scatter.6
  1432.6 358.8 all-reduce.4
where the time goes:
time: 1810 us
  local copies, waits for them, and re-layouts  780 us (43%)
  waiting for transfers between devices  517 us (29%)
  matrix products  295 us (16%)
  other arithmetic  143 us (8%)
  blocking collectives  59.9 us (3%)
    gather x11, local copies, waits for them, and re-layouts, pick_rows(): return jnp.take(matrix, indices, axis=0)  463 us
    psum x1, waiting for transfers between devices, per_device(): lax.psum((grad_query_weights, grad_value_weights, grad_output, grad_up, g...  341 us
    dot_general x1, matrix products, per_device(): jnp.einsum('rchij,rcihd->rcjhd', grad_scores, query_sorted, preferred_ele...  95 us
    dot_general x1, matrix products, per_device(): jnp.einsum('rchij,rcjhd->rcihd', grad_scores, key_window, preferred_eleme...  91.2 us
    reduce_scatter x1, waiting for transfers between devices, per_device(): lax.psum_scatter(jnp.dot(merged, output_proj, preferred_element_type=FLOA...  61.1 us
    unnamed x172, local copies, waits for them, and re-layouts  54.6 us
    reshape x3, local copies, waits for them, and re-layouts, restore(): sorted_grad.reshape(round_count, length, head_count, HD)  54.3 us
    gather x1, local copies, waits for them, and re-layouts, per_device(): jnp.take(value_rows, orderings, axis=0).reshape(sorted_shape)  41.9 us
  transfers between devices with their start and end apart: 9, of which 6 were waited for; matrix products, arithmetic and copies ran while one was open for 6% of the time, Pallas kernels for 0%

commit v1 on v0

v1 whole, which is shorter than its diff:
```python
from functools import partial
import math

import jax
import jax.numpy as jnp
from jax import lax
from jax.experimental import pallas as pl
from jax.experimental.pallas import tpu as pltpu
from jax.sharding import PartitionSpec as P

HD = 128
GROUP = 64
NB = 24
MOST = 768
BLOCK = 256
LANES = 128

FLOAT = jnp.float32
HALF = jnp.bfloat16
NEG = -1e30
EXP_SCALE = math.log2(math.e) / math.sqrt(HD)
FACTOR = 1.0 / math.sqrt(HD)


def normalize(inputs):
    center = inputs - jnp.mean(inputs, axis=-1, keepdims=True)
    inverse = lax.rsqrt(jnp.mean(center * center, axis=-1, keepdims=True) + 1e-05)
    return (center * inverse, inverse)


def norm_back(grad_out, scaled, inverse, gain):
    spread = grad_out * gain
    return inverse * (
        spread
        - jnp.mean(spread, axis=-1, keepdims=True)
        - scaled * jnp.mean(spread * scaled, axis=-1, keepdims=True)
    )


def contract_rows(left, right):
    return lax.dot_general(left, right, (((0,), (0,)), ((), ())), preferred_element_type=FLOAT)


def times_transpose(left, right):
    return lax.dot_general(left, right, (((1,), (1,)), ((), ())), preferred_element_type=FLOAT)


def one_hot(values, depth):
    return values[..., None] == jnp.arange(depth, dtype=jnp.int32)


def pair_features(orderings, doc_lengths):
    rounds, length = orderings.shape
    blocks = length // GROUP
    docs = doc_lengths.shape[0]
    places = jnp.arange(length, dtype=jnp.int32)
    high = one_hot(orderings // LANES, length // LANES).astype(HALF)
    low = jnp.where(one_hot(orderings % LANES, LANES), (places // GROUP)[None, :, None], 0).astype(HALF)
    group = jnp.einsum("rpa,rpb->rab", high, low, preferred_element_type=FLOAT)
    group = group.reshape(rounds, length).astype(jnp.int32).T
    ends = jnp.sum(
        jnp.where(jnp.arange(docs)[None, :] <= jnp.arange(docs)[:, None], doc_lengths[None, :], 0), axis=1
    )
    segment = jnp.sum((places[:, None] >= ends[None, :]).astype(jnp.int32), axis=-1)
    begins = jnp.sum(jnp.where(one_hot(segment, docs), (ends - doc_lengths)[None, :], 0), axis=-1)
    own = one_hot(group, blocks)
    before = one_hot((group + 1) % blocks, blocks)
    same = one_hot(segment, docs)
    width = rounds * blocks + docs
    pad = -width % LANES
    query = jnp.concatenate(
        [own.reshape(length, -1).astype(HALF), same.astype(HALF) * (2 * rounds), jnp.zeros((length, pad), HALF)], axis=1
    )
    key = jnp.concatenate(
        [(own | before).reshape(length, -1).astype(HALF), same.astype(HALF), jnp.zeros((length, pad), HALF)], axis=1
    )
    first = begins.reshape(length // BLOCK, BLOCK)[:, 0] // BLOCK
    return query, key, first.astype(jnp.int32)


def pair_counts(query, key, rounds, diagonal):
    total = times_transpose(query, key)
    counts = jnp.maximum(total - 2.0 * rounds, 0.0)
    if diagonal:
        rows = lax.broadcasted_iota(jnp.int32, counts.shape, 0)
        columns = lax.broadcasted_iota(jnp.int32, counts.shape, 1)
        counts = jnp.where(columns < rows, counts, 0.0)
    return counts


def attention_kernel(rounds, heads, steps, first, q_ref, k_ref, v_ref, fq_ref, fk_ref, merged_ref, logs_ref, counts, scores, peak, total, mixed):
    block = pl.program_id(0)
    size = q_ref.shape[0]

    def active(step):
        return (block - step) >= first[block]

    def rows(step):
        return pl.ds(pl.multiple_of((block - step) * size, size), size)

    for step in range(steps):

        @pl.when(active(step))
        def _():
            counts[step] = pair_counts(fq_ref[...], fk_ref[rows(step), :], rounds, step == 0)

    lane = lax.broadcasted_iota(jnp.int32, logs_ref.shape, 1)
    logs = jnp.zeros(logs_ref.shape, FLOAT)
    for head in range(heads):
        span = slice(head * HD, (head + 1) * HD)
        for step in range(steps):

            @pl.when(active(step))
            def _():
                raw = times_transpose(q_ref[:, span], k_ref[rows(step), span])
                raw = jnp.where(counts[step] > 0.0, raw, NEG)
                scores[step] = raw
                if step == 0:
                    peak[...] = raw
                else:
                    peak[...] = jnp.maximum(peak[...], raw)

        largest = jnp.max(peak[...], axis=-1, keepdims=True)
        for step in range(steps):

            @pl.when(active(step))
            def _():
                powers = counts[step] * jnp.exp2((scores[step] - largest) * EXP_SCALE)
                part = jnp.dot(powers.astype(HALF), v_ref[rows(step), span], preferred_element_type=FLOAT)
                if step == 0:
                    total[...] = powers
                    mixed[...] = part
                else:
                    total[...] += powers
                    mixed[...] += part

        sums = jnp.sum(total[...], axis=-1, keepdims=True)
        alone = sums == 0.0
        own = v_ref[rows(0), span].astype(FLOAT)
        result = jnp.where(alone, own, mixed[...] / jnp.where(alone, 1.0, sums))
        merged_ref[:, span] = result.astype(HALF)
        log_sum = jnp.where(alone, -NEG, largest * EXP_SCALE + jnp.log2(jnp.where(alone, 1.0, sums)))
        logs = jnp.where(lane == head, log_sum, logs)
    logs_ref[...] = logs


def attention(queries, keys, values, features, rounds):
    length, width = queries.shape
    heads = width // HD
    query_features, key_features, first = features
    depth = query_features.shape[1]
    steps = min(-(-(MOST - 1) // BLOCK), length // BLOCK - 1) + 1
    whole = lambda i, first: (0, 0)
    by_block = lambda i, first: (i, 0)
    return pl.pallas_call(
        partial(attention_kernel, rounds, heads, steps),
        grid_spec=pltpu.PrefetchScalarGridSpec(
            num_scalar_prefetch=1,
            grid=(length // BLOCK,),
            in_specs=[
                pl.BlockSpec((BLOCK, width), by_block),
                pl.BlockSpec((length, width), whole),
                pl.BlockSpec((length, width), whole),
                pl.BlockSpec((BLOCK, depth), by_block),
                pl.BlockSpec((length, depth), whole),
            ],
            out_specs=[
                pl.BlockSpec((BLOCK, width), by_block),
                pl.BlockSpec((BLOCK, LANES), by_block),
            ],
            scratch_shapes=[
                pltpu.VMEM((steps, BLOCK, BLOCK), FLOAT),
                pltpu.VMEM((steps, BLOCK, BLOCK), FLOAT),
                pltpu.VMEM((BLOCK, BLOCK), FLOAT),
                pltpu.VMEM((BLOCK, BLOCK), FLOAT),
                pltpu.VMEM((BLOCK, HD), FLOAT),
            ],
        ),
        out_shape=[
            jax.ShapeDtypeStruct((length, width), HALF),
            jax.ShapeDtypeStruct((length, LANES), FLOAT),
        ],
        compiler_params=pltpu.CompilerParams(vmem_limit_bytes=32 << 20),
        cost_estimate=pl.CostEstimate(flops=3 * 10**9, bytes_accessed=6 * 2**20, transcendentals=2 * 10**6),
        name="attention_forward",
    )(first, queries, keys, values, query_features, key_features)


def attention_back_kernel(
    rounds, heads, steps, first, q_ref, g_ref, merged_ref, logs_ref, fq_ref, fk_ref, k_ref, v_ref, all_q_ref, all_g_ref, all_logs_ref,
    grad_q_ref, grad_v_ref, counts, dq, dk, dv,
):
    block = pl.program_id(0)
    size = q_ref.shape[0]
    length = k_ref.shape[0]

    @pl.when(block == 0)
    def _():
        dk[...] = jnp.zeros_like(dk)
        dv[...] = jnp.zeros_like(dv)

    def active(step):
        return (block - step) >= first[block]

    def rows(step):
        return pl.ds(pl.multiple_of((block - step) * size, size), size)

    for step in range(steps):

        @pl.when(active(step))
        def _():
            counts[step] = pair_counts(fq_ref[...], fk_ref[rows(step), :], rounds, step == 0)

    for head in range(heads):
        span = slice(head * HD, (head + 1) * HD)
        log_sum = logs_ref[:, head : head + 1]
        along = jnp.sum(
            g_ref[:, span].astype(FLOAT) * merged_ref[:, span].astype(FLOAT), axis=-1, keepdims=True
        )
        for step in range(steps):

            @pl.when(active(step))
            def _():
                at = rows(step)
                raw = times_transpose(q_ref[:, span], k_ref[at, span])
                count = counts[step]
                weights = count * jnp.exp2(jnp.where(count > 0.0, raw * EXP_SCALE - log_sum, NEG))
                grad_probs = times_transpose(g_ref[:, span], v_ref[at, span])
                grad_scores = (weights * (grad_probs - along)).astype(HALF)
                dv[at, span] += contract_rows(weights.astype(HALF), g_ref[:, span])
                dk[at, span] += contract_rows(grad_scores, q_ref[:, span])
                part = jnp.dot(grad_scores, k_ref[at, span], preferred_element_type=FLOAT)
                here = rows(0)
                if step == 0:
                    dq[here, span] = part
                else:
                    dq[here, span] += part

    @pl.when(block == pl.num_programs(0) - 1)
    def _():
        @pl.loop(0, length // size)
        def _(index):
            at = pl.ds(pl.multiple_of(index * size, size), size)
            for head in range(heads):
                span = slice(head * HD, (head + 1) * HD)
                alone = all_logs_ref[at, head : head + 1] == -NEG
                grad_v_ref[at, span] = (
                    dv[at, span] + jnp.where(alone, all_g_ref[at, span].astype(FLOAT), 0.0)
                ).astype(HALF)
                query = all_q_ref[at, span].astype(FLOAT)
                key_scale = lax.rsqrt(jnp.sum(query * query, axis=-1, keepdims=True) + 1e-06)
                unit = query * key_scale
                grad_key = dk[at, span] * FACTOR
                key_along = jnp.sum(grad_key * unit, axis=-1, keepdims=True)
                grad_q_ref[at, span] = (
                    dq[at, span] * FACTOR + key_scale * (grad_key - unit * key_along)
                ).astype(HALF)


def attention_back(queries, keys, values, grads, merged, logs, features, rounds):
    length, width = queries.shape
    heads = width // HD
    query_features, key_features, first = features
    depth = query_features.shape[1]
    steps = min(-(-(MOST - 1) // BLOCK), length // BLOCK - 1) + 1
    whole = lambda i, first: (0, 0)
    by_block = lambda i, first: (i, 0)
    return pl.pallas_call(
        partial(attention_back_kernel, rounds, heads, steps),
        grid_spec=pltpu.PrefetchScalarGridSpec(
            num_scalar_prefetch=1,
            grid=(length // BLOCK,),
            in_specs=[
                pl.BlockSpec((BLOCK, width), by_block),
                pl.BlockSpec((BLOCK, width), by_block),
                pl.BlockSpec((BLOCK, width), by_block),
                pl.BlockSpec((BLOCK, LANES), by_block),
                pl.BlockSpec((BLOCK, depth), by_block),
                pl.BlockSpec((length, depth), whole),
                pl.BlockSpec((length, width), whole),
                pl.BlockSpec((length, width), whole),
                pl.BlockSpec((length, width), whole),
                pl.BlockSpec((length, width), whole),
                pl.BlockSpec((length, LANES), whole),
            ],
            out_specs=[pl.BlockSpec((length, width), whole), pl.BlockSpec((length, width), whole)],
            scratch_shapes=[
                pltpu.VMEM((steps, BLOCK, BLOCK), FLOAT),
                pltpu.VMEM((length, width), FLOAT),
                pltpu.VMEM((length, width), FLOAT),
                pltpu.VMEM((length, width), FLOAT),
            ],
        ),
        out_shape=[jax.ShapeDtypeStruct((length, width), HALF), jax.ShapeDtypeStruct((length, width), HALF)],
        compiler_params=pltpu.CompilerParams(vmem_limit_bytes=40 << 20),
        cost_estimate=pl.CostEstimate(flops=6 * 10**9, bytes_accessed=8 * 2**20, transcendentals=2 * 10**6),
        name="attention_backward",
    )(first, queries, grads, merged, logs, query_features, key_features, keys, values, queries, grads, logs)


def per_device(
    stream_one,
    stream_two,
    attention_gain,
    attention_shift,
    query_proj,
    value_proj,
    output_proj,
    forward_gain,
    forward_shift,
    up_proj,
    up_bias,
    down_proj,
    down_bias,
    bucket_ids,
    sort_orders,
    doc_lengths,
    cotan_one,
    cotan_two,
):
    gather = partial(lax.all_gather, axis_name="narrow", axis=0, tiled=True)
    scatter = partial(lax.psum_scatter, axis_name="narrow", scatter_dimension=0, tiled=True)
    first_rows = stream_one.astype(FLOAT)
    second_rows = stream_two.astype(FLOAT)
    orderings = sort_orders[0]
    rounds, length = orderings.shape
    heads = query_proj.shape[1] // HD

    scaled_one, inverse_one = normalize(second_rows)
    normed_one = (scaled_one * attention_gain + attention_shift).astype(HALF)
    gathered_one = gather(normed_one)
    grad_out_two = gather(cotan_two)
    features = pair_features(orderings, doc_lengths[0])
    queries = jnp.dot(gathered_one, query_proj, preferred_element_type=FLOAT).astype(HALF)
    by_head = queries.astype(FLOAT).reshape(length, heads, HD)
    key_scale = lax.rsqrt(jnp.sum(by_head * by_head, axis=-1, keepdims=True) + 1e-06)
    keys = (by_head * key_scale).astype(HALF).reshape(length, heads * HD)
    values = jnp.dot(gathered_one, value_proj, preferred_element_type=FLOAT).astype(HALF)
    merged, logs = attention(queries, keys, values, features, rounds)
    attended = scatter(jnp.dot(merged, output_proj, preferred_element_type=FLOAT).astype(HALF)).astype(FLOAT)
    middle = first_rows + attended
    scaled_two, inverse_two = normalize(middle)
    normed_two = (scaled_two * forward_gain + forward_shift).astype(HALF)
    gathered_two = gather(normed_two)
    hidden = jnp.dot(gathered_two, up_proj, preferred_element_type=FLOAT) + up_bias
    active_float, gelu_back = jax.vjp(partial(jax.nn.gelu, approximate=True), hidden)
    active = active_float.astype(HALF)
    grad_hidden = gelu_back(times_transpose(grad_out_two, down_proj))[0].astype(HALF)
    grad_normed_two = scatter(times_transpose(grad_hidden, up_proj).astype(HALF)).astype(FLOAT)
    grad_middle = cotan_one.astype(FLOAT) + norm_back(grad_normed_two, scaled_two, inverse_two, forward_gain)
    grad_first_low = grad_middle.astype(HALF)
    grad_rows = gather(grad_first_low)
    grad_down = contract_rows(active, grad_out_two)
    grad_down_bias = jnp.sum(grad_out_two, axis=0, dtype=FLOAT)
    grad_up = contract_rows(gathered_two, grad_hidden)
    grad_up_bias = jnp.sum(grad_hidden, axis=0, dtype=FLOAT)
    forward_sums = lax.psum((grad_up.astype(HALF), grad_down.astype(HALF)), "wide")
    fed_rows = scatter(jnp.dot(active, down_proj, preferred_element_type=FLOAT).astype(HALF)).astype(FLOAT)
    result_two = second_rows + (fed_rows + down_bias)
    grad_output = contract_rows(merged, grad_rows)
    grad_merged = times_transpose(grad_rows, output_proj).astype(HALF)
    grad_query, grad_value = attention_back(queries, keys, values, grad_merged, merged, logs, features, rounds)
    grad_query_weights = contract_rows(gathered_one, grad_query)
    grad_value_weights = contract_rows(gathered_one, grad_value)
    grad_normed_one = scatter(
        (times_transpose(grad_query, query_proj) + times_transpose(grad_value, value_proj)).astype(HALF)
    ).astype(FLOAT)
    grad_second = cotan_two.astype(FLOAT) + norm_back(grad_normed_one, scaled_one, inverse_one, attention_gain)
    attention_sums = lax.psum(
        (grad_query_weights.astype(HALF), grad_value_weights.astype(HALF), grad_output.astype(HALF)), "wide"
    )
    levels = jnp.arange(NB, dtype=jnp.int32)
    counts = jnp.sum((bucket_ids[:, :, None] == levels).astype(FLOAT), axis=0)
    norm_totals = lax.psum(
        (
            jnp.sum(grad_normed_one * scaled_one, axis=0),
            jnp.sum(grad_normed_one, axis=0),
            jnp.sum(grad_normed_two * scaled_two, axis=0),
            jnp.sum(grad_normed_two, axis=0),
            counts,
        ),
        ("wide", "narrow"),
    )
    bias_sums = lax.psum((grad_up_bias, grad_down_bias), "wide")
    return (
        middle.astype(HALF),
        result_two.astype(HALF),
        grad_first_low,
        grad_second.astype(HALF),
        norm_totals[0],
        norm_totals[1],
        attention_sums[0].astype(FLOAT),
        attention_sums[1].astype(FLOAT),
        attention_sums[2].astype(FLOAT),
        norm_totals[2],
        norm_totals[3],
        forward_sums[0].astype(FLOAT),
        bias_sums[0],
        forward_sums[1].astype(FLOAT),
        bias_sums[1],
        norm_totals[4].astype(jnp.int32),
    )


def solution(mesh):
    rows = P(("wide", "narrow"), None)
    columns = P(None, "narrow")
    return jax.shard_map(
        per_device,
        mesh=mesh,
        in_specs=(
            rows,
            rows,
            P(),
            P(),
            columns,
            columns,
            P("narrow", None),
            P(),
            P(),
            columns,
            P("narrow"),
            P("narrow", None),
            P(),
            rows,
            P("wide", None, None),
            P("wide", None),
            rows,
            rows,
        ),
        out_specs=(
            rows,
            rows,
            rows,
            rows,
            P(),
            P(),
            columns,
            columns,
            P("narrow", None),
            P(),
            P(),
            columns,
            P("narrow"),
            P("narrow", None),
            P(),
            P(),
        ),
        check_vma=False,
    )
```

time: 1810 us -> 607 us (0.34)
  local copies, waits for them, and re-layouts: 780 us -> 13.4 us
  matrix products: 295 us -> 71.6 us
  waiting for transfers between devices: 517 us -> 352 us
  other arithmetic: 143 us -> 45.5 us
  Pallas kernels: 0 us -> 39 us
    gather x16 -> x0, local copies, waits for them, and re-layouts: 621 us -> none  [the longest x11 463 us: pick_rows(): return jnp.take(matrix, indices, axis=0)]
    dot_general x8 -> x3, matrix products: 233 us -> 12.8 us  [the longest x1 8.94 us: per_device(): jnp.dot(active, down_proj, preferred_element_type=FLOAT).astype(HALF)]
    psum x1, waiting for transfers between devices: 341 us -> 162 us  [per_device(): lax.psum((grad_query_weights.astype(HALF), grad_value_weights.astype(HALF...]
    reshape x7 -> x1, local copies, waits for them, and re-layouts: 77.7 us -> 0.01 us  [pair_features(): first = begins.reshape(length // BLOCK, BLOCK)[:, 0] // BLOCK]
    reduce_sum x9 -> x4, other arithmetic: 74 us -> 5.33 us  [the longest x1 4.63 us: per_device(): jnp.sum(by_head * by_head, axis=-1, keepdims=True) + 1e-06]
    unnamed x172 -> x78, local copies, waits for them, and re-layouts: 54.6 us -> 6.76 us
    pallas_call x0 -> x2, Pallas kernels: none -> 39 us  [the longest x1 22.1 us: attention_back(): pl.pallas_call(partial(attention_back_kernel, rounds, heads, steps), grid...]
  transfers between devices with their start and end apart: 9 -> 9, of which waited for: 6 -> 8; matrix products, arithmetic and copies ran while one was open for 6% -> 10% of each run, Pallas kernels for 0% -> 0%
where the time goes in v1:
time: 607 us; the launch traced here: 597 us
  waiting for transfers between devices  352 us (58%)
  matrix products  71.6 us (12%)
  blocking collectives  59.7 us (10%)
  other arithmetic  45.5 us (7%)
  Pallas kernels  39 us (6%)
  between operations  14.8 us (2%)
  local copies, waits for them, and re-layouts  13.4 us (2%)
    psum x1, waiting for transfers between devices, per_device(): lax.psum((grad_query_weights.astype(HALF), grad_value_weights.astype(HALF...  162 us
    psum x1, blocking collectives, per_device(): lax.psum((jnp.sum(grad_normed_one * scaled_one, axis=0), jnp.sum(grad_nor...  39.8 us
    reduce_scatter x1, waiting for transfers between devices, per_device(): scatter(times_transpose(grad_hidden, up_proj).astype(HALF)).astype(FLOAT)  38.1 us
    reduce_scatter x1, waiting for transfers between devices, per_device(): scatter(jnp.dot(merged, output_proj, preferred_element_type=FLOAT).astype...  36.7 us
    reduce_scatter x1, waiting for transfers between devices, per_device(): scatter((times_transpose(grad_query, query_proj) + times_transpose(grad_v...  28.9 us
    all_gather x1, waiting for transfers between devices, per_device(): gathered_two = gather(normed_two)  28 us
    all_gather x1, waiting for transfers between devices, per_device(): gathered_one = gather(normed_one)  24.2 us
    dot_general x5, matrix products, times_transpose(): lax.dot_general(left, right, (((1,), (1,)), ((), ())), preferred_element_...  22.7 us
  transfers between devices with their start and end apart: 9, of which 8 were waited for; matrix products, arithmetic and copies ran while one was open for 10% of the time, Pallas kernels for 0%

profile of v1, /device:TPU:0, one launch (start us, length us, event | category | flops | bytes accessed | tf_op | source)
XLA Modules:
  0.0 596.9 jit_solution(1802641695227493056)
XLA Ops:
  10.2 2.4 fusion.18
  19.8 24.2 %all-gather.5.cloned.1.call-done = bf16[1536,1024]{1,0:T(8,128)(2,1)} async-done(((bf16[384,1024]{1,0:T(8,128)(2,1)}), bf16[1536,1024]{1,0:T(8,128)(2,1)}) %all-gather.5.cloned.1.call-update) | async-done | bytes 3145744 | tf_op jit(solution)/shard_map/all_gather | solution.py:331
  44.0 4.1 convert_multiply_fusion.5
  48.1 2.9 mul.163
  51.0 4.6 reduce_sum.179
  60.4 16.9 %attention_forward.1 = (bf16[1536,256]{1,0:T(8,128)(2,1)S(1)}, f32[1536,128]{1,0:T(8,128)S(1)}) custom-call(s32[6]{0:T(128)S(1)} %and_select_fusion.first, bf16[1536,256]{1,0:T(8,128)(2,1)S(1)} %get-tuple-element.59.q_ref.all_q_ref, bf16[1536,256]{1,0:T(8,128)(2,1)S(1)} %fusion.24.k_ref, bf16[1536,256]{1,0:T(8,128)(2,1)S(1)} %convolution_convert_fusion.4.v_ref, ...), custom_call_target="tpu_custom_call" | custom-call | flops 3000000000 | bytes 6291456 | tf_op jit(solution)/shard_map/attention_forward/pallas_call | solution.py:155
  78.2 2.6 convolution_convert_fusion
  82.3 36.7 %reduce-scatter.5.cloned.1.call-done = bf16[384,1024]{1,0:T(8,128)(2,1)} async-done(((bf16[1536,1024]{1,0:T(8,128)(2,1)}), bf16[384,1024]{1,0:T(8,128)(2,1)}) %reduce-scatter.5.cloned.1.call-update) | async-done | bytes 786448 | tf_op jit(solution)/shard_map/reduce_scatter | solution.py:340
  124.5 28.0 %all-gather.7.cloned.1.call-done = bf16[1536,1024]{1,0:T(8,128)(2,1)} async-done(((bf16[384,1024]{1,0:T(8,128)(2,1)}), bf16[1536,1024]{1,0:T(8,128)(2,1)}) %all-gather.7.cloned.1.call-update) | async-done | bytes 3145744 | tf_op jit(solution)/shard_map/all_gather | solution.py:344
  152.6 8.6 %fusion.53 = f32[1536,1024]{1,0:T(8,128)} fusion(bf16[1536,1024]{1,0:T(8,128)(2,1)} %all-gather.7.cloned.1.call-done, bf16[1024,1024]{1,0:T(8,128)(2,1)} %param.27), kind=kOutput, calls=%fused_computation.129 | convolution fusion | flops 3221225472 | bytes 11534336 | tf_op jit(solution)/shard_map/dot_general | solution.py:345
  161.2 21.4 %all-gather.9.cloned.1.call-done = bf16[1536,1024]{1,0:T(8,128)(2,1)} async-done(((bf16[384,1024]{1,0:T(8,128)(2,1)}), bf16[1536,1024]{1,0:T(8,128)(2,1)}) %all-gather.9.cloned.1.call-update) | async-done | bytes 3145744 | tf_op jit(solution)/shard_map/all_gather | solution.py:332
  182.6 10.8 %convert_reduce_fusion.1 = (f32[1024]{0:T(1024)S(1)}, bf16[1536,1024]{1,0:T(8,128)(2,1)S(1)}) fusion(f32[1536,1024]{1,0:T(8,128)} %fusion.53, f32[1024]{0:T(1024)S(1)} %copy-done.36, bf16[1536,1024]{1,0:T(8,128)(2,1)} %all-gather.9.cloned.1.call-done, bf16[1024,1024]{1,0:T(8,128)(2,1)S(1)} %copy-done), kind=kOutput, calls=%fused_computation.10 | convolution fusion | flops 3257400320 | bytes 14688256 | tf_op jit(solution)/shard_map/dot_general | solution.py:45
  195.1 4.9 convolution_convert_fusion.1
  200.1 38.1 %reduce-scatter.9.cloned.1.call-done = bf16[384,1024]{1,0:T(8,128)(2,1)} async-done(((bf16[1536,1024]{1,0:T(8,128)(2,1)}), bf16[384,1024]{1,0:T(8,128)(2,1)}) %reduce-scatter.9.cloned.1.call-update) | async-done | bytes 786448 | tf_op jit(solution)/shard_map/reduce_scatter | solution.py:349
  238.2 2.5 fusion.32
  240.6 3.7 fusion.29
  244.6 7.8 %convolution_convert_fusion.7 = bf16[1024,1024]{1,0:T(8,128)(2,1)} fusion(bf16[1536,1024]{1,0:T(8,128)(2,1)} %all-gather.7.cloned.1.call-done, bf16[1536,1024]{1,0:T(8,128)(2,1)} %copy-done.38), kind=kOutput, calls=%fused_computation.39 | convolution fusion | flops 3222274048 | bytes 8388608 | tf_op jit(solution)/shard_map/dot_general | solution.py:41
  252.4 9.0 %convolution_convert_fusion.6 = bf16[1024,1024]{1,0:T(8,128)(2,1)} fusion(bf16[1536,1024]{1,0:T(8,128)(2,1)S(1)} %copy-done.20, f32[1536,1024]{1,0:T(8,128)} %fusion.53, f32[1024]{0:T(1024)S(1)} %copy-done.36), kind=kOutput, calls=%fused_computation.38 | convolution fusion | flops 3238002688 | bytes 11538432 | tf_op jit(solution)/shard_map/dot_general | solution.py:41
  261.4 11.6 %all-gather.11.cloned.1.call-done = bf16[1536,1024]{1,0:T(8,128)(2,1)} async-done(((bf16[384,1024]{1,0:T(8,128)(2,1)}), bf16[1536,1024]{1,0:T(8,128)(2,1)}) %all-gather.11.cloned.1.call-update) | async-done | bytes 3145744 | tf_op jit(solution)/shard_map/all_gather | solution.py:352
  273.0 3.2 convolution_convert_fusion.3.g_ref.all_g_ref
  276.3 22.1 %attention_backward.1 = (bf16[1536,256]{1,0:T(8,128)(2,1)S(1)}, bf16[1536,256]{1,0:T(8,128)(2,1)S(1)}) custom-call(s32[6]{0:T(128)S(1)} %and_select_fusion.first, bf16[1536,256]{1,0:T(8,128)(2,1)S(1)} %get-tuple-element.59.q_ref.all_q_ref, bf16[1536,256]{1,0:T(8,128)(2,1)S(1)} %convolution_convert_fusion.3.g_ref.all_g_ref, bf16[1536,256]{1,0:T(8,128)(2,1)S(1)} %copy-done.2, ...), custom_call_target="tpu_custom_call" | custom-call | flops 6000000000 | bytes 8388608 | tf_op jit(solution)/shard_map/attention_backward/pallas_call | solution.py:268
  307.3 2.9 add_convert_fusion
  310.5 8.9 %convolution_convert_fusion.2 = bf16[1536,1024]{1,0:T(8,128)(2,1)} fusion(bf16[1024,1024]{1,0:T(8,128)(2,1)S(1)} %copy-done, f32[1536,1024]{1,0:T(8,128)} %fusion.53, f32[1024]{0:T(1024)S(1)} %copy-done.36), kind=kOutput, calls=%fused_computation.15 | convolution fusion | flops 3238526976 | bytes 11538432 | tf_op jit(solution)/shard_map/dot_general | solution.py:358
  320.3 2.5 convert_reduce_fusion
  322.7 19.8 %all-reduce.1 = (f32[1024]{0:T(1024)}, f32[1024]{0:T(1024)}) all-reduce(f32[1024]{0:T(1024)S(1)} %get-tuple-element.44, f32[1024]{0:T(1024)S(1)} %convert_reduce_fusion), channel_id=1, replica_groups=mesh['wide'=8,'narrow'=4] {'wide'}, use_global_device_ids=true, to_apply=%region_29.30 | all-reduce | flops 2048 | bytes 16384 | tf_op jit(solution)/shard_map/psum | solution.py:384
  342.6 162.1 %all-reduce.5.cloned.1.call-done = (bf16[1024,256]{1,0:T(8,128)(2,1)}, bf16[1024,256]{1,0:T(8,128)(2,1)}, bf16[256,1024]{1,0:T(8,128)(2,1)}, bf16[1024,1024]{1,0:T(8,128)(2,1)}, bf16[1024,1024]{1,0:T(8,128)(2,1)}) async-done(((bf16[1024,256]{1,0:T(8,128)(2,1)}, bf16[1024,256]{1,0:T(8,128)(2,1)}, bf16[256,1024]{1,0:T(8,128)(2,1)}, bf16[1024,1024]{1,0:T(8,128)(2,1)}, bf16[1024,1024]{1,0:T(8,128)(2,1)}), ...) | async-done | bytes 5767184 | tf_op jit(solution)/shard_map/psum | solution.py:369
  504.7 2.2 convert_element_type.174
  510.1 2.5 convert_element_type.180
  512.6 2.6 convert_element_type.183
  515.1 28.9 %reduce-scatter.11.cloned.1.call-done = bf16[384,1024]{1,0:T(8,128)(2,1)} async-done(((bf16[1536,1024]{1,0:T(8,128)(2,1)}), bf16[384,1024]{1,0:T(8,128)(2,1)}) %reduce-scatter.11.cloned.1.call-update) | async-done | bytes 786448 | tf_op jit(solution)/shard_map/reduce_scatter | solution.py:365
  546.0 39.8 %all-reduce = (f32[1024]{0:T(1024)}, f32[1024]{0:T(1024)}, f32[1024]{0:T(1024)}, f32[1024]{0:T(1024)}, f32[4,24]{1,0:T(4,128)S(1)}) all-reduce(f32[1024]{0:T(1024)S(1)} %get-tuple-element.26, f32[1024]{0:T(1024)S(1)} %get-tuple-element.31, f32[1024]{0:T(1024)S(1)} %get-tuple-element.24, ...), channel_id=1, replica_groups=mesh['wide'=8,'narrow'=4] {'wide','narrow'}, use_global_device_ids=true, to_apply=%region_17.18 | all-reduce | flops 4192 | bytes 33536 | tf_op jit(solution)/shard_map/psum | solution.py:374
  586.4 3.5 fusion.22
  (146 shorter events, 40.2 us)
Async XLA Ops:
  7.2 175.5 %copy-start = (bf16[1024,1024]{1,0:T(8,128)(2,1)S(1)}, bf16[1024,1024]{1,0:T(8,128)(2,1)}, u32[]{:S(2)}) copy-start(bf16[1024,1024]{1,0:T(8,128)(2,1)} %param.29) | copy-start | bytes 6291460
  7.2 5.6 copy-start.37
  7.2 6.3 %copy-start.30 = (s32[1,4,1536]{2,1,0:T(4,128)S(1)}, s32[1,4,1536]{2,1,0:T(4,128)}, u32[]{:S(2)}) copy-start(s32[1,4,1536]{2,1,0:T(4,128)} %param.32) | copy-start | bytes 73732
  7.2 36.8 %all-gather.5.cloned.1.call-start = ((), (), s32[]{:S(2)}) async-start(), calls=%async_computation.4 | async-start | bytes 3932160 | tf_op jit(solution)/shard_map/all_gather | solution.py:331
  12.6 106.4 %reduce-scatter.5.cloned.1.call-start = ((), (), s32[]{:S(2)}) async-start(), calls=%async_computation.5 | async-start | bytes 3932160 | tf_op jit(solution)/shard_map/reduce_scatter | solution.py:340
  60.2 17.2 %copy-start.11 = (bf16[1536,256]{1,0:T(8,128)(2,1)}, bf16[1536,256]{1,0:T(8,128)(2,1)S(1)}, u32[]{:S(2)}) copy-start(bf16[1536,256]{1,0:T(8,128)(2,1)S(1)} %convolution_convert_fusion.4.v_ref) | copy-start | bytes 2359300
  60.4 17.8 %copy-start.24 = (bf16[256,1024]{1,0:T(8,128)(2,1)S(1)}, bf16[256,1024]{1,0:T(8,128)(2,1)}, u32[]{:S(2)}) copy-start(bf16[256,1024]{1,0:T(8,128)(2,1)} %param.24) | copy-start | bytes 1572868
  81.7 40.8 %copy-start.29 = (f32[1024]{0:T(1024)S(1)}, f32[1024]{0:T(1024)}, u32[]{:S(2)}) copy-start(f32[1024]{0:T(1024)} %param.25) | copy-start | bytes 12292
  81.7 40.8 %copy-start.32 = (f32[1024]{0:T(1024)S(1)}, f32[1024]{0:T(1024)}, u32[]{:S(2)}) copy-start(f32[1024]{0:T(1024)} %param.26) | copy-start | bytes 12292
  81.8 70.8 %all-gather.7.cloned.1.call-start = ((), (), s32[]{:S(2)}) async-start(), calls=%async_computation.6 | async-start | bytes 3932160 | tf_op jit(solution)/shard_map/all_gather | solution.py:344
  119.0 3.6 copy-start.16
  119.0 3.6 copy-start.17
  123.9 58.7 %all-gather.9.cloned.1.call-start = ((), (), s32[]{:S(2)}) async-start(), calls=%async_computation.8 | async-start | bytes 3932160 | tf_op jit(solution)/shard_map/all_gather | solution.py:332
  124.5 58.2 %copy-start.36 = (f32[1024]{0:T(1024)S(1)}, f32[1024]{0:T(1024)}, u32[]{:S(2)}) copy-start(f32[1024]{0:T(1024)} %param.28) | copy-start | bytes 12292
  124.5 113.7 %reduce-scatter.9.cloned.1.call-start = ((), (), s32[]{:S(2)}) async-start(), calls=%async_computation.9 | async-start | bytes 3932160 | tf_op jit(solution)/shard_map/reduce_scatter | solution.py:349
  182.6 12.5 %copy-start.35 = (bf16[1024,1024]{1,0:T(8,128)(2,1)S(1)}, bf16[1024,1024]{1,0:T(8,128)(2,1)}, u32[]{:S(2)}) copy-start(bf16[1024,1024]{1,0:T(8,128)(2,1)} %param.27) | copy-start | bytes 6291460
  200.1 73.0 %all-gather.11.cloned.1.call-start = ((), (), s32[]{:S(2)}) async-start(), calls=%async_computation.10 | async-start | bytes 3932160 | tf_op jit(solution)/shard_map/all_gather | solution.py:352
  244.3 260.3 %all-reduce.5.cloned.1.call-start = ((), (), s32[]{:S(2)}) async-start(), calls=%async_computation.12 | async-start | bytes 11534336 | tf_op jit(solution)/shard_map/psum | solution.py:369
  244.5 7.8 %copy-start.20 = (bf16[1536,1024]{1,0:T(8,128)(2,1)S(1)}, bf16[1536,1024]{1,0:T(8,128)(2,1)}, u32[]{:S(2)}) copy-start(bf16[1536,1024]{1,0:T(8,128)(2,1)} %all-gather.9.cloned.1.call-done) | copy-start | bytes 9437188
  273.0 3.2 copy-start.10
  273.0 3.2 copy-start.12
  273.0 3.2 copy-start.14
  276.2 22.2 %copy-start.34 = (bf16[1536,1024]{1,0:T(8,128)(2,1)S(1)}, bf16[1536,1024]{1,0:T(8,128)(2,1)}, u32[]{:S(2)}) copy-start(bf16[1536,1024]{1,0:T(8,128)(2,1)} %all-gather.11.cloned.1.call-done) | copy-start | bytes 9437188
  298.4 4.5 copy-start.3
  298.4 4.5 copy-start.7
  304.8 239.3 %reduce-scatter.11.cloned.1.call-start = ((), (), s32[]{:S(2)}) async-start(), calls=%async_computation.11 | async-start | bytes 3932160 | tf_op jit(solution)/shard_map/reduce_scatter | solution.py:365
  310.2 276.2 %reduce-scatter.7.cloned.1.call-start = ((), (), s32[]{:S(2)}) async-start(), calls=%async_computation.7 | async-start | bytes 3932160 | tf_op jit(solution)/shard_map/reduce_scatter | solution.py:358
  504.6 4.3 copy-start.25
  504.6 5.4 copy-start.22
  512.6 31.5 %copy-start.15 = (bf16[384,1024]{1,0:T(8,128)(2,1)S(1)}, bf16[384,1024]{1,0:T(8,128)(2,1)}, u32[]{:S(2)}) copy-start(bf16[384,1024]{1,0:T(8,128)(2,1)} %param.19) | copy-start | bytes 2359300
  512.6 31.5 %copy-start.28 = (f32[1024]{0:T(1024)S(1)}, f32[1024]{0:T(1024)}, u32[]{:S(2)}) copy-start(f32[1024]{0:T(1024)} %param.20) | copy-start | bytes 12292
  512.6 73.9 %copy-start.33 = (f32[1024]{0:T(1024)S(1)}, f32[1024]{0:T(1024)}, u32[]{:S(2)}) copy-start(f32[1024]{0:T(1024)} %param.30) | copy-start | bytes 12292
  (16 other events, 27.2 us)
Sparse Core Ops, SparseCore 0:
  12.7 31.2 all-gather.4
  81.9 37.0 reduce-scatter.4
  124.0 28.5 all-gather.6
  154.1 28.5 all-gather.8
  200.2 37.9 reduce-scatter.8
  244.4 28.5 all-gather.10
  304.9 199.6 all-reduce.4
  507.3 36.7 reduce-scatter.10
  546.6 38.2 reduce-scatter.6

commit v2 on v1

v2 whole, which is shorter than its diff:
```python
from functools import partial
import math

import jax
import jax.numpy as jnp
from jax import lax
from jax.experimental import pallas as pl
from jax.experimental.pallas import tpu as pltpu
from jax.sharding import PartitionSpec as P

HD = 128
GROUP = 64
NB = 24
MOST = 768
BLOCK = 256
LANES = 128
CHUNK = 128
NARROW = 4

FLOAT = jnp.float32
HALF = jnp.bfloat16
NEG = -1e30
EXP_SCALE = math.log2(math.e) / math.sqrt(HD)
FACTOR = 1.0 / math.sqrt(HD)
MESH = pl.DeviceIdType.MESH
IN_VMEM = pl.BlockSpec(memory_space=pltpu.VMEM)
IN_SMEM = pl.BlockSpec(memory_space=pltpu.SMEM)
ANYWHERE = pl.BlockSpec(memory_space=pl.ANY)
DMA = pltpu.SemaphoreType.DMA


def normalize(inputs):
    center = inputs - jnp.mean(inputs, axis=-1, keepdims=True)
    inverse = lax.rsqrt(jnp.mean(center * center, axis=-1, keepdims=True) + 1e-05)
    return (center * inverse, inverse)


def norm_back(grad_out, scaled, inverse, gain):
    spread = grad_out * gain
    return inverse * (
        spread
        - jnp.mean(spread, axis=-1, keepdims=True)
        - scaled * jnp.mean(spread * scaled, axis=-1, keepdims=True)
    )


def contract_rows(left, right):
    return lax.dot_general(left, right, (((0,), (0,)), ((), ())), preferred_element_type=FLOAT)


def times_transpose(left, right):
    return lax.dot_general(left, right, (((1,), (1,)), ((), ())), preferred_element_type=FLOAT)


def times(left, right):
    return jnp.dot(left, right, preferred_element_type=FLOAT)


def column_sums(rows):
    return times(jnp.ones((8, rows.shape[0]), rows.dtype), rows)[0:1]


class Place:
    def __init__(self):
        index = lax.axis_index("narrow")
        core, chip = lax.rem(index, 2), lax.div(index, 2)
        self.me = index
        self.near = 2 * chip + 1 - core
        self.far = 2 * (1 - chip) + core
        self.cross = 2 * (1 - chip) + 1 - core


def span(start, size):
    return pl.ds(pl.multiple_of(start, size), size)


def meet(place):
    barrier = pltpu.get_barrier_semaphore()
    for other in (place.near, place.far):
        pl.semaphore_signal(barrier, inc=1, device_id={"narrow": other}, device_id_type=MESH)
    pl.semaphore_wait(barrier, 2)


def remote(source, target, sent, arrived, other):
    return pltpu.make_async_remote_copy(
        src_ref=source,
        dst_ref=target,
        send_sem=sent,
        recv_sem=arrived,
        device_id={"narrow": other},
        device_id_type=MESH,
    )


class Gather:
    def __init__(self, place, whole, rows, sems):
        self.place, self.whole, self.rows = place, whole, rows
        self.sent, self.arrived = sems
        self.chunks = rows // CHUNK

    def at(self, owner, chunk):
        return self.whole.at[span(owner * self.rows + chunk * CHUNK, CHUNK), :]

    def copy(self, lane, owner, chunk, other):
        index = lane * self.chunks + chunk
        piece = self.at(owner, chunk)
        return remote(piece, piece, self.sent.at[index], self.arrived.at[index], other)

    def to_far(self, chunk):
        return self.copy(0, self.place.me, chunk, self.place.far)

    def to_near(self, chunk):
        return self.copy(1, self.place.me, chunk, self.place.near)

    def onward(self, chunk):
        return self.copy(2, self.place.far, chunk, self.place.near)

    def send(self, chunk):
        self.to_far(chunk).start()
        self.to_near(chunk).start()

    def take_near(self, chunk):
        self.to_near(chunk).wait_recv()

    def take_far(self, chunk):
        self.to_far(chunk).wait_recv()
        self.onward(chunk).start()

    def take_cross(self, chunk):
        self.onward(chunk).wait_recv()

    def finish(self):
        @pl.loop(0, self.chunks)
        def _(chunk):
            self.to_far(chunk).wait_send()
            self.to_near(chunk).wait_send()
            self.onward(chunk).wait_send()


def gather_sems(rows):
    return [DMA((3 * (rows // CHUNK),)), DMA((3 * (rows // CHUNK),))]


class Scatter:
    def __init__(self, place, term, rows, buffers, sems):
        self.place, self.term, self.rows = place, term, rows
        self.near_out, self.near_in, self.far_out, self.far_in = buffers
        self.sent, self.arrived = sems
        self.chunks = rows // CHUNK

    def to_near(self, part, chunk):
        index = part * self.chunks + chunk
        at = span(chunk * CHUNK, CHUNK)
        return remote(
            self.near_out.at[part, at, :],
            self.near_in.at[part, at, :],
            self.sent.at[index],
            self.arrived.at[index],
            self.place.near,
        )

    def to_far(self, chunk):
        index = 2 * self.chunks + chunk
        at = span(chunk * CHUNK, CHUNK)
        return remote(
            self.far_out.at[at, :], self.far_in.at[at, :], self.sent.at[index], self.arrived.at[index], self.place.far
        )

    def part(self, owner, chunk):
        return self.term(span(owner * self.rows + chunk * CHUNK, CHUNK))

    def start(self):
        @pl.loop(0, self.chunks)
        def _(chunk):
            self.near_out[0, span(chunk * CHUNK, CHUNK), :] = self.part(self.place.cross, chunk).astype(HALF)
            self.to_near(0, chunk).start()

        @pl.loop(0, self.chunks)
        def _(chunk):
            at = span(chunk * CHUNK, CHUNK)
            own = self.part(self.place.far, chunk)
            self.to_near(0, chunk).wait_recv()
            self.far_out[at, :] = (own + self.near_in[0, at, :].astype(FLOAT)).astype(HALF)
            self.to_far(chunk).start()

        @pl.loop(0, self.chunks)
        def _(chunk):
            self.near_out[1, span(chunk * CHUNK, CHUNK), :] = self.part(self.place.near, chunk).astype(HALF)
            self.to_near(1, chunk).start()

    def chip_sum(self, chunk):
        own = self.part(self.place.me, chunk)
        self.to_near(1, chunk).wait_recv()
        return own + self.near_in[1, span(chunk * CHUNK, CHUNK), :].astype(FLOAT)

    def take_far(self, chunk):
        self.to_far(chunk).wait_recv()
        return self.far_in[span(chunk * CHUNK, CHUNK), :].astype(FLOAT)

    def finish(self):
        @pl.loop(0, self.chunks)
        def _(chunk):
            self.to_near(0, chunk).wait_send()
            self.to_near(1, chunk).wait_send()
            self.to_far(chunk).wait_send()


def scatter_buffers(rows, width):
    return [
        pltpu.VMEM((2, rows, width), HALF),
        pltpu.VMEM((2, rows, width), HALF),
        pltpu.VMEM((rows, width), HALF),
        pltpu.VMEM((rows, width), HALF),
    ]


def scatter_sems(rows):
    return [DMA((3 * (rows // CHUNK),)), DMA((3 * (rows // CHUNK),))]


def fetch(copies, sems):
    handles = [pltpu.make_async_copy(source, target, sems.at[i]) for i, (source, target) in enumerate(copies)]
    for handle in handles:
        handle.start()
    return handles


def call(kernel, outs, ins, args, scratch, collective, flops, moved):
    return pl.pallas_call(
        kernel,
        out_shape=[jax.ShapeDtypeStruct(*o) for o in outs],
        in_specs=ins,
        out_specs=[IN_VMEM] * len(outs),
        scratch_shapes=scratch,
        compiler_params=pltpu.CompilerParams(
            collective_id=collective, has_side_effects=True, vmem_limit_bytes=58 << 20
        ),
        cost_estimate=pl.CostEstimate(flops=flops, bytes_accessed=moved, transcendentals=0),
        name=kernel.__name__,
    )(*args)


def pair_features(orders, docs, query_features, key_features, work_q, work_k):
    rounds, length = orders.shape
    groups = length // GROUP
    high_count = length // LANES
    high_rows = -(-high_count // 8) * 8
    count = docs.shape[0]
    lane = lax.broadcasted_iota(jnp.int32, (LANES, length), 1)
    low_at = lax.broadcasted_iota(jnp.int32, (LANES, length), 0)
    high_at = lax.broadcasted_iota(jnp.int32, (high_rows, length), 0)
    group_at = lax.broadcasted_iota(jnp.int32, (groups, LANES), 0).astype(FLOAT)
    sorted_group = lax.shift_right_logical(lane, int(math.log2(GROUP))).astype(FLOAT)
    work_q[...] = jnp.zeros_like(work_q)
    work_k[...] = jnp.zeros_like(work_k)
    for index in range(rounds):
        row = orders[index : index + 1, :]
        high = jnp.where(high_at == lax.shift_right_logical(row, int(math.log2(LANES))), 1.0, 0.0)
        low = jnp.where(low_at == (row & (LANES - 1)), sorted_group, 0.0)
        group = times_transpose(high.astype(HALF), low.astype(HALF))
        for block in range(high_count):
            own = group[block : block + 1, :]
            after = jnp.where(own == groups - 1.0, 0.0, own + 1.0)
            at = slice(block * LANES, (block + 1) * LANES)
            rows = slice(index * groups, (index + 1) * groups)
            mine = group_at == own
            work_q[rows, at] = jnp.where(mine, 1.0, 0.0)
            work_k[rows, at] = jnp.where(mine | (group_at == after), 1.0, 0.0)
    place = lax.broadcasted_iota(jnp.int32, (count, length), 1)
    which = lax.broadcasted_iota(jnp.int32, (count, length), 0)
    same = jnp.zeros((count, length), FLOAT)
    begin = jnp.int32(0)
    for doc in range(count):
        end = begin + docs[doc]
        same = jnp.where((which == doc) & (place >= begin) & (place < end), 1.0, same)
        begin = end
    work_q[rounds * groups : rounds * groups + count, :] = same * (2.0 * rounds)
    work_k[rounds * groups : rounds * groups + count, :] = same
    query_features[...] = work_q[...].astype(HALF)
    key_features[...] = work_k[...].astype(HALF)


def project_in(
    rows_ref, gain, shift, wq_any, wv_any, orders, docs, buckets,
    whole, queries, keys, values, query_features, key_features, bucket_sums,
    wq, wv, work_q, work_k, loads, sent, arrived,
):
    place = Place()
    rows = rows_ref.shape[0]
    weights = fetch([(wq_any, wq), (wv_any, wv)], loads)
    meet(place)
    gather = Gather(place, whole, rows, (sent, arrived))

    @pl.loop(0, gather.chunks)
    def _(chunk):
        scaled, _ = normalize(rows_ref[span(chunk * CHUNK, CHUNK), :].astype(FLOAT))
        normed = (scaled * gain[...] + shift[...]).astype(HALF)
        whole[span(place.me * rows + chunk * CHUNK, CHUNK), :] = normed
        gather.send(chunk)

    pair_features(orders, docs, query_features, key_features, work_q, work_k)
    level = lax.broadcasted_iota(jnp.int32, (rows, LANES), 1)
    sums = [
        jnp.sum(jnp.where(level == buckets[:, index : index + 1], 1.0, 0.0), axis=0, keepdims=True)
        for index in range(buckets.shape[1])
    ]
    sums += [jnp.zeros((1, LANES), FLOAT)] * (8 - len(sums))
    bucket_sums[...] = jnp.concatenate(sums, axis=0)
    for weight in weights:
        weight.wait()

    def project(owner):
        at = span(owner * rows, rows)
        query = times(whole[at, :], wq[...]).astype(HALF)
        queries[at, :] = query
        for head in range(query.shape[1] // HD):
            part = query[:, head * HD : (head + 1) * HD].astype(FLOAT)
            scale = lax.rsqrt(jnp.sum(part * part, axis=-1, keepdims=True) + 1e-06)
            keys[at, head * HD : (head + 1) * HD] = (part * scale).astype(HALF)
        values[at, :] = times(whole[at, :], wv[...]).astype(HALF)

    @pl.loop(0, NARROW)
    def _(step):
        @pl.loop(0, gather.chunks)
        def _(chunk):
            @pl.when(step == 1)
            def _():
                gather.take_near(chunk)

            @pl.when(step == 2)
            def _():
                gather.take_far(chunk)

            @pl.when(step == 3)
            def _():
                gather.take_cross(chunk)

        project(in_turn(place, step))

    gather.finish()


def in_turn(place, step):
    flip_core, flip_chip = lax.rem(step, 2), lax.div(step, 2)
    core, chip = lax.rem(place.me, 2), lax.div(place.me, 2)
    core = core + flip_core * (1 - 2 * core)
    chip = chip + flip_chip * (1 - 2 * chip)
    return 2 * chip + core


def run_project_in(rows, gain, shift, wq, wv, orders, docs, buckets):
    count, width = rows.shape
    length = NARROW * count
    heads = wq.shape[1]
    depth = -(-(orders.shape[0] * (length // GROUP) + docs.shape[0]) // LANES) * LANES
    return call(
        project_in,
        [
            ((length, width), HALF),
            ((length, heads), HALF),
            ((length, heads), HALF),
            ((length, heads), HALF),
            ((depth, length), HALF),
            ((depth, length), HALF),
            ((8, LANES), FLOAT),
        ],
        [IN_VMEM, IN_VMEM, IN_VMEM, ANYWHERE, ANYWHERE, IN_VMEM, IN_SMEM, IN_VMEM],
        (rows, gain, shift, wq, wv, orders, docs, buckets),
        [
            pltpu.VMEM(wq.shape, HALF),
            pltpu.VMEM(wv.shape, HALF),
            pltpu.VMEM((depth, length), FLOAT),
            pltpu.VMEM((depth, length), FLOAT),
            DMA((2,)),
            *gather_sems(count),
        ],
        0,
        4 * length * width * heads,
        10 << 20,
    )


def doc_start(docs, position):
    start = jnp.int32(0)
    begin = jnp.int32(0)
    for doc in range(docs.shape[0]):
        start = jnp.where(position >= begin, begin, start)
        begin = begin + docs[doc]
    return start


def pair_counts(query, key, rounds, diagonal):
    total = contract_rows(query, key)
    counts = jnp.maximum(total - 2.0 * rounds, 0.0)
    if diagonal:
        rows = lax.broadcasted_iota(jnp.int32, counts.shape, 0)
        columns = lax.broadcasted_iota(jnp.int32, counts.shape, 1)
        counts = jnp.where(columns < rows, counts, 0.0)
    return counts


def attention_forward(rounds, heads, steps, docs, q_ref, k_ref, v_ref, fq_ref, fk_ref, merged_ref, logs_ref, counts, scores, peak, total, mixed):
    block = pl.program_id(0)
    size = q_ref.shape[0]
    first = lax.div(doc_start(docs, block * size), size)

    def active(step):
        return (block - step) >= first

    def rows(step):
        return span((block - step) * size, size)

    for step in range(steps):

        @pl.when(active(step))
        def _():
            counts[step] = pair_counts(fq_ref[...], fk_ref[:, rows(step)], rounds, step == 0)

    lane = lax.broadcasted_iota(jnp.int32, logs_ref.shape, 1)
    logs = jnp.zeros(logs_ref.shape, FLOAT)
    for head in range(heads):
        part_of = slice(head * HD, (head + 1) * HD)
        for step in range(steps):

            @pl.when(active(step))
            def _():
                raw = times_transpose(q_ref[:, part_of], k_ref[rows(step), part_of])
                raw = jnp.where(counts[step] > 0.0, raw, NEG)
                scores[step] = raw
                if step == 0:
                    peak[...] = raw
                else:
                    peak[...] = jnp.maximum(peak[...], raw)

        largest = jnp.max(peak[...], axis=-1, keepdims=True)
        for step in range(steps):

            @pl.when(active(step))
            def _():
                powers = counts[step] * jnp.exp2((scores[step] - largest) * EXP_SCALE)
                part = times(powers.astype(HALF), v_ref[rows(step), part_of])
                if step == 0:
                    total[...] = powers
                    mixed[...] = part
                else:
                    total[...] += powers
                    mixed[...] += part

        sums = jnp.sum(total[...], axis=-1, keepdims=True)
        alone = sums == 0.0
        own = v_ref[rows(0), part_of].astype(FLOAT)
        result = jnp.where(alone, own, mixed[...] / jnp.where(alone, 1.0, sums))
        merged_ref[:, part_of] = result.astype(HALF)
        log_sum = jnp.where(alone, -NEG, largest * EXP_SCALE + jnp.log2(jnp.where(alone, 1.0, sums)))
        logs = jnp.where(lane == head, log_sum, logs)
    logs_ref[...] = logs


def band_steps(length):
    return min(-(-(MOST - 1) // BLOCK), length // BLOCK - 1) + 1


def run_attention(queries, keys, values, query_features, key_features, docs, rounds):
    length, width = queries.shape
    depth = query_features.shape[0]
    steps = band_steps(length)
    whole = lambda i, docs: (0, 0)
    by_block = lambda i, docs: (i, 0)
    return pl.pallas_call(
        partial(attention_forward, rounds, width // HD, steps),
        grid_spec=pltpu.PrefetchScalarGridSpec(
            num_scalar_prefetch=1,
            grid=(length // BLOCK,),
            in_specs=[
                pl.BlockSpec((BLOCK, width), by_block),
                pl.BlockSpec((length, width), whole),
                pl.BlockSpec((length, width), whole),
                pl.BlockSpec((depth, BLOCK), lambda i, docs: (0, i)),
                pl.BlockSpec((depth, length), whole),
            ],
            out_specs=[
                pl.BlockSpec((BLOCK, width), by_block),
                pl.BlockSpec((BLOCK, LANES), by_block),
            ],
            scratch_shapes=[
                pltpu.VMEM((steps, BLOCK, BLOCK), FLOAT),
                pltpu.VMEM((steps, BLOCK, BLOCK), FLOAT),
                pltpu.VMEM((BLOCK, BLOCK), FLOAT),
                pltpu.VMEM((BLOCK, BLOCK), FLOAT),
                pltpu.VMEM((BLOCK, HD), FLOAT),
            ],
        ),
        out_shape=[
            jax.ShapeDtypeStruct((length, width), HALF),
            jax.ShapeDtypeStruct((length, LANES), FLOAT),
        ],
        compiler_params=pltpu.CompilerParams(vmem_limit_bytes=32 << 20),
        cost_estimate=pl.CostEstimate(flops=6 * 10**9, bytes_accessed=6 * 2**20, transcendentals=2 * 10**6),
        name="attention_forward",
    )(docs, queries, keys, values, query_features, key_features)


def attention_backward(
    rounds, heads, steps, docs, q_ref, g_ref, merged_ref, logs_ref, fq_ref, fk_ref, k_ref, v_ref, all_q_ref, all_g_ref, all_logs_ref,
    grad_q_ref, grad_v_ref, counts, dq, dk, dv,
):
    block = pl.program_id(0)
    size = q_ref.shape[0]
    length = k_ref.shape[0]
    first = lax.div(doc_start(docs, block * size), size)

    @pl.when(block == 0)
    def _():
        dk[...] = jnp.zeros_like(dk)
        dv[...] = jnp.zeros_like(dv)

    def active(step):
        return (block - step) >= first

    def rows(step):
        return span((block - step) * size, size)

    for step in range(steps):

        @pl.when(active(step))
        def _():
            counts[step] = pair_counts(fq_ref[...], fk_ref[:, rows(step)], rounds, step == 0)

    for head in range(heads):
        part_of = slice(head * HD, (head + 1) * HD)
        log_sum = logs_ref[:, head : head + 1]
        along = jnp.sum(
            g_ref[:, part_of].astype(FLOAT) * merged_ref[:, part_of].astype(FLOAT), axis=-1, keepdims=True
        )
        for step in range(steps):

            @pl.when(active(step))
            def _():
                at = rows(step)
                raw = times_transpose(q_ref[:, part_of], k_ref[at, part_of])
                count = counts[step]
                weights = count * jnp.exp2(jnp.where(count > 0.0, raw * EXP_SCALE - log_sum, NEG))
                grad_probs = times_transpose(g_ref[:, part_of], v_ref[at, part_of])
                grad_scores = (weights * (grad_probs - along)).astype(HALF)
                dv[at, part_of] += contract_rows(weights.astype(HALF), g_ref[:, part_of])
                dk[at, part_of] += contract_rows(grad_scores, q_ref[:, part_of])
                part = times(grad_scores, k_ref[at, part_of])
                here = rows(0)
                if step == 0:
                    dq[here, part_of] = part
                else:
                    dq[here, part_of] += part

    @pl.when(block == pl.num_programs(0) - 1)
    def _():
        @pl.loop(0, length // size)
        def _(index):
            at = span(index * size, size)
            for head in range(heads):
                part_of = slice(head * HD, (head + 1) * HD)
                alone = all_logs_ref[at, head : head + 1] == -NEG
                grad_v_ref[at, part_of] = (
                    dv[at, part_of] + jnp.where(alone, all_g_ref[at, part_of].astype(FLOAT), 0.0)
                ).astype(HALF)
                query = all_q_ref[at, part_of].astype(FLOAT)
                key_scale = lax.rsqrt(jnp.sum(query * query, axis=-1, keepdims=True) + 1e-06)
                unit = query * key_scale
                grad_key = dk[at, part_of] * FACTOR
                key_along = jnp.sum(grad_key * unit, axis=-1, keepdims=True)
                grad_q_ref[at, part_of] = (
                    dq[at, part_of] * FACTOR + key_scale * (grad_key - unit * key_along)
                ).astype(HALF)


def run_attention_back(queries, keys, values, grads, merged, logs, query_features, key_features, docs, rounds):
    length, width = queries.shape
    depth = query_features.shape[0]
    steps = band_steps(length)
    whole = lambda i, docs: (0, 0)
    by_block = lambda i, docs: (i, 0)
    return pl.pallas_call(
        partial(attention_backward, rounds, width // HD, steps),
        grid_spec=pltpu.PrefetchScalarGridSpec(
            num_scalar_prefetch=1,
            grid=(length // BLOCK,),
            in_specs=[
                pl.BlockSpec((BLOCK, width), by_block),
                pl.BlockSpec((BLOCK, width), by_block),
                pl.BlockSpec((BLOCK, width), by_block),
                pl.BlockSpec((BLOCK, LANES), by_block),
                pl.BlockSpec((depth, BLOCK), lambda i, docs: (0, i)),
                pl.BlockSpec((depth, length), whole),
                pl.BlockSpec((length, width), whole),
                pl.BlockSpec((length, width), whole),
                pl.BlockSpec((length, width), whole),
                pl.BlockSpec((length, width), whole),
                pl.BlockSpec((length, LANES), whole),
            ],
            out_specs=[pl.BlockSpec((length, width), whole), pl.BlockSpec((length, width), whole)],
            scratch_shapes=[
                pltpu.VMEM((steps, BLOCK, BLOCK), FLOAT),
                pltpu.VMEM((length, width), FLOAT),
                pltpu.VMEM((length, width), FLOAT),
                pltpu.VMEM((length, width), FLOAT),
            ],
        ),
        out_shape=[jax.ShapeDtypeStruct((length, width), HALF), jax.ShapeDtypeStruct((length, width), HALF)],
        compiler_params=pltpu.CompilerParams(vmem_limit_bytes=40 << 20),
        cost_estimate=pl.CostEstimate(flops=10**10, bytes_accessed=8 * 2**20, transcendentals=2 * 10**6),
        name="attention_backward",
    )(docs, queries, grads, merged, logs, query_features, key_features, keys, values, queries, grads, logs)


def feed_in(
    merged, wo, first_rows, gain, shift, up_any, up_bias, down_any, cotan_own, cotan_far,
    out_one, middle, whole, cotans, active, grad_hidden,
    up, down, near_out, near_in, far_out, far_in, loads, cotan_sent, cotan_arrived, sent, arrived, gather_sent, gather_arrived,
):
    place = Place()
    rows, width = first_rows.shape
    weights = fetch([(down_any, down), (up_any, up)], loads)
    own_at, far_at = span(place.me * rows, rows), span(place.far * rows, rows)
    local = [
        pltpu.make_async_copy(cotan_own, cotans.at[own_at, :], loads.at[2]),
        pltpu.make_async_copy(cotan_far, cotans.at[far_at, :], loads.at[3]),
    ]
    for copy in local:
        copy.start()
    meet(place)
    spread = [
        remote(cotan_own, cotans.at[own_at, :], cotan_sent.at[0], cotan_arrived.at[0], place.near),
        remote(cotan_far, cotans.at[far_at, :], cotan_sent.at[1], cotan_arrived.at[1], place.near),
    ]
    for copy in spread:
        copy.start()
    scatter = Scatter(
        place, lambda at: times(merged[at, :], wo[...]), rows, (near_out, near_in, far_out, far_in), (sent, arrived)
    )
    gather = Gather(place, whole, rows, (gather_sent, gather_arrived))
    scatter.start()

    @pl.loop(0, scatter.chunks)
    def _(chunk):
        at = span(chunk * CHUNK, CHUNK)
        middle[at, :] = first_rows[at, :].astype(FLOAT) + scatter.chip_sum(chunk)

    weights[0].wait()
    for copy in local + spread:
        copy.wait()

    def back(owner):
        @pl.loop(0, 2)
        def _(half):
            at = span(half * (width // 2), width // 2)
            grad_hidden[span(owner * rows, rows), at] = times_transpose(
                cotans[span(owner * rows, rows), :], down[at, :]
            ).astype(HALF)

    @pl.loop(0, NARROW)
    def _(owner):
        back(owner)

    @pl.loop(0, scatter.chunks)
    def _(chunk):
        at = span(chunk * CHUNK, CHUNK)
        value = middle[at, :] + scatter.take_far(chunk)
        middle[at, :] = value
        out_one[at, :] = value.astype(HALF)
        scaled, _ = normalize(value)
        whole[span(place.me * rows + chunk * CHUNK, CHUNK), :] = (scaled * gain[...] + shift[...]).astype(HALF)
        gather.send(chunk)

    weights[1].wait()

    @pl.loop(0, NARROW)
    def _(step):
        @pl.loop(0, gather.chunks)
        def _(chunk):
            @pl.when(step == 1)
            def _():
                gather.take_near(chunk)

            @pl.when(step == 2)
            def _():
                gather.take_far(chunk)

            @pl.when(step == 3)
            def _():
                gather.take_cross(chunk)

        owner = in_turn(place, step)
        row_at = span(owner * rows, rows)

        @pl.loop(0, 2)
        def _(half):
            at = span(half * (width // 2), width // 2)
            hidden = times(whole[row_at, :], up[:, at]) + up_bias[:, at]
            square = hidden * hidden
            inner = math.sqrt(2.0 / math.pi) * hidden * (1.0 + 0.044715 * square)
            bend = jnp.tanh(inner)
            half_more = 0.5 + 0.5 * bend
            active[row_at, at] = (hidden * half_more).astype(HALF)
            slope = half_more + 0.5 * hidden * (1.0 - bend * bend) * (
                math.sqrt(2.0 / math.pi) * (1.0 + 3.0 * 0.044715 * square)
            )
            grad_hidden[row_at, at] = (grad_hidden[row_at, at].astype(FLOAT) * slope).astype(HALF)

    scatter.finish()
    gather.finish()


def run_feed_in(merged, wo, first_rows, gain, shift, up, up_bias, down, cotan_own, cotan_far):
    rows, width = first_rows.shape
    length, hidden = NARROW * rows, up.shape[1]
    return call(
        feed_in,
        [
            ((rows, width), HALF),
            ((rows, width), FLOAT),
            ((length, width), HALF),
            ((length, width), HALF),
            ((length, hidden), HALF),
            ((length, hidden), HALF),
        ],
        [IN_VMEM] * 5 + [ANYWHERE, IN_VMEM, ANYWHERE, IN_VMEM, IN_VMEM],
        (merged, wo, first_rows, gain, shift, up, up_bias, down, cotan_own, cotan_far),
        [
            pltpu.VMEM(up.shape, HALF),
            pltpu.VMEM(down.shape, HALF),
            *scatter_buffers(rows, width),
            DMA((4,)),
            DMA((2,)),
            DMA((2,)),
            *scatter_sems(rows),
            *gather_sems(rows),
        ],
        1,
        4 * length * width * hidden,
        24 << 20,
    )


def feed_back(
    grad_hidden, up, middle, gain, cotan_one, active_any, down_any, cotans_any, whole_any, merged_any, wo_any,
    grad_one, grad_merged, grad_up, grad_down, grad_out, fed_own, fed_far, sums,
    active, down, cotans, whole, merged, wo, grad_rows, near_out, near_in, far_out, far_in, fed_out, fed_in,
    loads, sent, arrived, gather_sent, gather_arrived, fed_sent, fed_arrived,
):
    place = Place()
    rows, width = middle.shape
    handles = fetch(
        [(active_any, active), (cotans_any, cotans), (down_any, down), (whole_any, whole), (wo_any, wo), (merged_any, merged)],
        loads,
    )
    meet(place)
    scatter = Scatter(
        place,
        lambda at: times_transpose(grad_hidden[at, :], up[...]),
        rows,
        (near_out, near_in, far_out, far_in),
        (sent, arrived),
    )
    gather = Gather(place, grad_rows, rows, (gather_sent, gather_arrived))
    scatter.start()

    handles[0].wait()
    handles[1].wait()
    tiles(grad_down, active, cotans)
    handles[2].wait()

    def fed_copy(part, chunk):
        index = part * scatter.chunks + chunk
        at = span(chunk * CHUNK, CHUNK)
        return remote(fed_out.at[part, at, :], fed_in.at[part, at, :], fed_sent.at[index], fed_arrived.at[index], place.near)

    @pl.loop(0, scatter.chunks)
    def _(chunk):
        at = span(chunk * CHUNK, CHUNK)
        for part, owner in enumerate((place.cross, place.near)):
            fed_out[part, at, :] = times(active[span(owner * rows + chunk * CHUNK, CHUNK), :], down[...]).astype(HALF)
            fed_copy(part, chunk).start()

    totals = [jnp.zeros((1, width), FLOAT), jnp.zeros((1, width), FLOAT)]

    def back(chunk, totals):
        at = span(chunk * CHUNK, CHUNK)
        grad_normed = scatter.chip_sum(chunk) + scatter.take_far(chunk)
        scaled, inverse = normalize(middle[at, :])
        grad = cotan_one[at, :].astype(FLOAT) + norm_back(grad_normed, scaled, inverse, gain[...])
        low = grad.astype(HALF)
        grad_one[at, :] = low
        grad_rows[span(place.me * rows + chunk * CHUNK, CHUNK), :] = low
        gather.send(chunk)
        return [
            totals[0] + jnp.sum(grad_normed * scaled, axis=0, keepdims=True),
            totals[1] + jnp.sum(grad_normed, axis=0, keepdims=True),
        ]

    totals = lax.fori_loop(0, scatter.chunks, back, totals)

    @pl.loop(0, scatter.chunks)
    def _(chunk):
        at = span(chunk * CHUNK, CHUNK)
        for part, (owner, target) in enumerate(((place.far, fed_far), (place.me, fed_own))):
            own = times(active[span(owner * rows + chunk * CHUNK, CHUNK), :], down[...])
            fed_copy(part, chunk).wait_recv()
            target[at, :] = (own + fed_in[part, at, :].astype(FLOAT)).astype(HALF)

    handles[3].wait()
    tiles(grad_up, whole, grad_hidden)
    sums[...] = jnp.concatenate(
        [*totals, column_sums(grad_hidden[...]), column_sums(cotans[...]), jnp.zeros((4, width), FLOAT)], axis=0
    )
    handles[4].wait()

    @pl.loop(0, NARROW)
    def _(step):
        @pl.loop(0, gather.chunks)
        def _(chunk):
            @pl.when(step == 1)
            def _():
                gather.take_near(chunk)

            @pl.when(step == 2)
            def _():
                gather.take_far(chunk)

            @pl.when(step == 3)
            def _():
                gather.take_cross(chunk)

        at = span(in_turn(place, step) * rows, rows)
        grad_merged[at, :] = times_transpose(grad_rows[at, :], wo[...]).astype(HALF)

    handles[5].wait()
    grad_out[...] = contract_rows(merged[...], grad_rows[...]).astype(HALF)
    scatter.finish()
    gather.finish()

    @pl.loop(0, scatter.chunks)
    def _(chunk):
        fed_copy(0, chunk).wait_send()
        fed_copy(1, chunk).wait_send()


def tiles(result, left, right):
    width = 256

    @pl.loop(0, left.shape[1] // width)
    def _(index):
        at = span(index * width, width)
        result[at, :] = contract_rows(left[:, at], right[...]).astype(result.dtype)


def run_feed_back(grad_hidden, up, middle, gain, cotan_one, active, down, cotans, whole, merged, wo):
    rows, width = middle.shape
    length, hidden = grad_hidden.shape
    heads = merged.shape[1]
    return call(
        feed_back,
        [
            ((rows, width), HALF),
            ((length, heads), HALF),
            ((width, hidden), HALF),
            ((hidden, width), HALF),
            ((heads, width), HALF),
            ((rows, width), HALF),
            ((rows, width), HALF),
            ((8, width), FLOAT),
        ],
        [IN_VMEM] * 5 + [ANYWHERE] * 6,
        (grad_hidden, up, middle, gain, cotan_one, active, down, cotans, whole, merged, wo),
        [
            pltpu.VMEM(active.shape, HALF),
            pltpu.VMEM(down.shape, HALF),
            pltpu.VMEM(cotans.shape, HALF),
            pltpu.VMEM(whole.shape, HALF),
            pltpu.VMEM(merged.shape, HALF),
            pltpu.VMEM(wo.shape, HALF),
            pltpu.VMEM((length, width), HALF),
            *scatter_buffers(rows, width),
            pltpu.VMEM((2, rows, width), HALF),
            pltpu.VMEM((2, rows, width), HALF),
            DMA((6,)),
            *scatter_sems(rows),
            *gather_sems(rows),
            DMA((2 * (rows // CHUNK),)),
            DMA((2 * (rows // CHUNK),)),
        ],
        2,
        8 * length * width * hidden,
        30 << 20,
    )


def project_back(
    grad_query, grad_value, wq, wv, whole_any, second_rows, gain, cotan_two, fed_own, fed_far, down_bias,
    out_two, grad_two, grad_weights, sums,
    whole, near_out, near_in, far_out, far_in, loads, sent, arrived,
):
    place = Place()
    rows, width = second_rows.shape
    heads = grad_query.shape[1]
    [load] = fetch([(whole_any, whole)], loads)
    meet(place)
    scatter = Scatter(
        place,
        lambda at: times_transpose(grad_query[at, :], wq[...]) + times_transpose(grad_value[at, :], wv[...]),
        rows,
        (near_out, near_in, far_out, far_in),
        (sent, arrived),
    )
    scatter.start()
    out_two[...] = (
        second_rows[...].astype(FLOAT) + (fed_own[...].astype(FLOAT) + fed_far[...].astype(FLOAT) + down_bias[...])
    ).astype(HALF)
    load.wait()

    @pl.loop(0, width // 256)
    def _(index):
        at = span(index * 256, 256)
        grad_weights[at, 0:heads] = contract_rows(whole[:, at], grad_query[...]).astype(HALF)
        grad_weights[at, heads : 2 * heads] = contract_rows(whole[:, at], grad_value[...]).astype(HALF)

    def back(chunk, totals):
        at = span(chunk * CHUNK, CHUNK)
        grad_normed = scatter.chip_sum(chunk) + scatter.take_far(chunk)
        scaled, inverse = normalize(second_rows[at, :].astype(FLOAT))
        grad_two[at, :] = (
            cotan_two[at, :].astype(FLOAT) + norm_back(grad_normed, scaled, inverse, gain[...])
        ).astype(HALF)
        return [
            totals[0] + jnp.sum(grad_normed * scaled, axis=0, keepdims=True),
            totals[1] + jnp.sum(grad_normed, axis=0, keepdims=True),
        ]

    totals = lax.fori_loop(
        0, scatter.chunks, back, [jnp.zeros((1, width), FLOAT), jnp.zeros((1, width), FLOAT)]
    )
    sums[...] = jnp.concatenate([*totals, jnp.zeros((6, width), FLOAT)], axis=0)
    scatter.finish()


def run_project_back(grad_query, grad_value, wq, wv, whole, second_rows, gain, cotan_two, fed_own, fed_far, down_bias):
    rows, width = second_rows.shape
    length, heads = grad_query.shape
    return call(
        project_back,
        [
            ((rows, width), HALF),
            ((rows, width), HALF),
            ((width, 2 * heads), HALF),
            ((8, width), FLOAT),
        ],
        [IN_VMEM] * 4 + [ANYWHERE] + [IN_VMEM] * 6,
        (grad_query, grad_value, wq, wv, whole, second_rows, gain, cotan_two, fed_own, fed_far, down_bias),
        [
            pltpu.VMEM((length, width), HALF),
            *scatter_buffers(rows, width),
            DMA((1,)),
            *scatter_sems(rows),
        ],
        3,
        8 * length * width * heads,
        14 << 20,
    )


def ring_place(members, index):
    column, row = lax.rem(index, 2), lax.div(index, 2)
    return row + column * (members - 1 - 2 * row)


def ring_member(members, place):
    back = lax.div(place, members // 2)
    return 2 * place + back * (2 * (members - 1 - place) + 1 - 2 * place)


def sum_wide(members, arrays, *refs):
    data, small_ins = refs[:arrays], refs[arrays : arrays + 3]
    results, small_out = refs[arrays + 3 : 2 * arrays + 3], refs[2 * arrays + 3]
    landed = refs[2 * arrays + 4 : 3 * arrays + 4]
    narrow_all, wide_all, sent, arrived, narrow_sent, narrow_arrived, wide_sent, wide_arrived = refs[3 * arrays + 4 :]
    wide, narrow = lax.axis_index("wide"), lax.axis_index("narrow")
    here = ring_place(members, wide)
    neighbours = (
        ring_member(members, lax.rem(here + 1, members)),
        ring_member(members, lax.rem(here + members - 1, members)),
    )
    barrier = pltpu.get_barrier_semaphore()

    @pl.loop(1, NARROW)
    def _(step):
        pl.semaphore_signal(
            barrier, inc=1, device_id={"narrow": lax.rem(narrow + step, NARROW)}, device_id_type=MESH
        )

    @pl.loop(1, members)
    def _(step):
        pl.semaphore_signal(barrier, inc=1, device_id={"wide": lax.rem(wide + step, members)}, device_id_type=MESH)

    pl.semaphore_wait(barrier, NARROW - 1 + members - 1)

    def piece(direction, step):
        if direction == 0:
            at = lax.rem(here - step + 2 * members, members)
        else:
            at = lax.rem(here + step, members)
        return 2 * at + direction

    def copy(kind, array, direction, step):
        source = (data, results)[kind][array]
        target = (landed, results)[kind][array]
        at = piece(direction, step)
        index = ((kind * 2 + direction) * arrays + array) * (members - 1) + (step - kind * (members - 1))
        return pltpu.make_async_remote_copy(
            src_ref=source.at[at],
            dst_ref=target.at[at],
            send_sem=sent.at[index],
            recv_sem=arrived.at[index],
            device_id={"wide": neighbours[direction]},
            device_id_type=MESH,
        )

    def landing(kind, array, direction, step):
        source = (data, results)[kind][array]
        target = (landed, results)[kind][array]
        at = piece(direction, step + 1)
        index = ((kind * 2 + direction) * arrays + array) * (members - 1) + (step - kind * (members - 1))
        return pltpu.make_async_remote_copy(
            src_ref=source.at[at],
            dst_ref=target.at[at],
            send_sem=sent.at[index],
            recv_sem=arrived.at[index],
            device_id={"wide": neighbours[direction]},
            device_id_type=MESH,
        )

    lanes = [(array, direction) for array in range(arrays) for direction in range(2)]
    for array, direction in lanes:
        copy(0, array, direction, 0).start()

    vectors = small_ins[0].shape[0]
    mine = narrow_all.at[narrow]
    narrow_all[narrow] = small_ins[0][...] + small_ins[1][...]

    def to_narrow(step):
        return pltpu.make_async_remote_copy(
            src_ref=mine,
            dst_ref=mine,
            send_sem=narrow_sent.at[step],
            recv_sem=narrow_arrived.at[step],
            device_id={"narrow": lax.rem(narrow + step, NARROW)},
            device_id_type=MESH,
        )

    for step in range(1, NARROW):
        to_narrow(step).start()
    for step in range(1, NARROW):
        to_narrow(step).wait()
    total = narrow_all[0]
    for index in range(1, NARROW):
        total = total + narrow_all[index]
    wide_all[wide] = total + small_ins[2][...]
    own = wide_all.at[wide]

    def to_wide(step):
        return pltpu.make_async_remote_copy(
            src_ref=own,
            dst_ref=own,
            send_sem=wide_sent.at[step],
            recv_sem=wide_arrived.at[step],
            device_id={"wide": lax.rem(wide + step, members)},
            device_id_type=MESH,
        )

    @pl.loop(1, members)
    def _(step):
        to_wide(step).start()

    @pl.loop(0, members - 2)
    def _(step):
        for array, direction in lanes:
            at = piece(direction, step + 1)
            landing(0, array, direction, step).wait_recv()
            data[array][at] = (data[array][at].astype(FLOAT) + landed[array][at].astype(FLOAT)).astype(HALF)
            copy(0, array, direction, step + 1).start()

    last = members - 1
    for array, direction in lanes:
        at = piece(direction, last)
        landing(0, array, direction, last - 1).wait_recv()
        results[array][at] = (data[array][at].astype(FLOAT) + landed[array][at].astype(FLOAT)).astype(HALF)
        copy(1, array, direction, last).start()

    @pl.loop(last, 2 * last - 1)
    def _(step):
        for array, direction in lanes:
            landing(1, array, direction, step).wait_recv()
            copy(1, array, direction, step + 1).start()

    for array, direction in lanes:
        landing(1, array, direction, 2 * last - 1).wait_recv()

    @pl.loop(1, members)
    def _(step):
        to_wide(step).wait()

    small_out[...] = jnp.zeros_like(small_out)

    @pl.loop(0, members)
    def _(index):
        small_out[...] += wide_all[index]

    @pl.loop(0, last)
    def _(step):
        for array, direction in lanes:
            copy(0, array, direction, step).wait_send()
            copy(1, array, direction, last + step).wait_send()


def run_sum_wide(members, arrays, narrow_small, narrow_more, wide_small):
    width = narrow_small.shape[1]
    shaped = []
    for array in arrays:
        size = array.size // (2 * members)
        columns = max(LANES, array.shape[1] * 8 // members)
        shaped.append(array.reshape(2 * members, size // columns, columns))
    copies = 4 * len(arrays) * (members - 1)
    results = call(
        partial_named(sum_wide, members, len(arrays)),
        [(a.shape, HALF) for a in shaped] + [((8, width), FLOAT)],
        [IN_VMEM] * (len(arrays) + 3),
        (*shaped, narrow_small, narrow_more, wide_small),
        [pltpu.VMEM(a.shape, HALF) for a in shaped]
        + [
            pltpu.VMEM((NARROW, 8, width), FLOAT),
            pltpu.VMEM((members, 8, width), FLOAT),
            DMA((copies,)),
            DMA((copies,)),
            DMA((NARROW,)),
            DMA((NARROW,)),
            DMA((members,)),
            DMA((members,)),
        ],
        4,
        10**6,
        24 << 20,
    )
    return [r.reshape(a.shape) for r, a in zip(results, arrays)], results[-1]


def partial_named(function, *args):
    bound = partial(function, *args)
    bound.__name__ = function.__name__
    return bound


def per_device(
    stream_one,
    stream_two,
    attention_gain,
    attention_shift,
    query_proj,
    value_proj,
    output_proj,
    forward_gain,
    forward_shift,
    up_proj,
    up_bias,
    down_proj,
    down_bias,
    bucket_ids,
    sort_orders,
    doc_lengths,
    cotan_one,
    cotan_two,
):
    members = lax.axis_size("wide")
    row = lambda vector: vector.reshape(1, -1)
    across = [(i, (i + NARROW // 2) % NARROW) for i in range(NARROW)]
    orders, docs = sort_orders[0], doc_lengths[0]
    rounds = orders.shape[0]
    gain_one, gain_two = row(attention_gain), row(forward_gain)

    gathered, queries, keys, values, query_features, key_features, bucket_sums = run_project_in(
        stream_two, gain_one, row(attention_shift), query_proj, value_proj, orders, docs, bucket_ids
    )
    cotan_two_later, queries = lax.optimization_barrier((cotan_two, queries))
    cotan_far = lax.ppermute(cotan_two_later, "narrow", across)
    merged, logs = run_attention(queries, keys, values, query_features, key_features, docs, rounds)
    out_one, middle, whole, cotans, active, grad_hidden = run_feed_in(
        merged, output_proj, stream_one, gain_two, row(forward_shift), up_proj, row(up_bias), down_proj, cotan_two, cotan_far
    )
    grad_one, grad_merged, grad_up, grad_down, grad_out, fed_own, fed_far, sums_two = run_feed_back(
        grad_hidden, up_proj, middle, gain_two, cotan_one, active, down_proj, cotans, whole, merged, output_proj
    )
    fed_other = lax.ppermute(fed_far, "narrow", across)
    grad_query, grad_value = run_attention_back(
        queries, keys, values, grad_merged, merged, logs, query_features, key_features, docs, rounds
    )
    out_two, grad_two, grad_weights, sums_one = run_project_back(
        grad_query, grad_value, query_proj, value_proj, gathered, stream_two, gain_one, cotan_two, fed_own, fed_other, row(down_bias)
    )
    width = stream_one.shape[1]
    bucket_row = bucket_sums[:rounds, :NB].reshape(1, -1)
    bucket_row = jnp.pad(bucket_row, ((0, 0), (0, width - bucket_row.shape[1])))
    blank = jnp.zeros((1, width), FLOAT)
    narrow_small = jnp.concatenate([sums_one[0:2], sums_two[0:2], bucket_row, blank, blank, blank], axis=0)
    wide_small = jnp.concatenate([blank] * 5 + [sums_two[2:4], blank], axis=0)
    (grad_up, grad_down, grad_out, grad_weights), small = run_sum_wide(
        members, [grad_up, grad_down, grad_out, grad_weights], narrow_small, jnp.zeros_like(narrow_small), wide_small
    )
    heads = query_proj.shape[1]
    return (
        out_one,
        out_two,
        grad_one,
        grad_two,
        small[0],
        small[1],
        grad_weights[:, :heads].astype(FLOAT),
        grad_weights[:, heads:].astype(FLOAT),
        grad_out.astype(FLOAT),
        small[2],
        small[3],
        grad_up.astype(FLOAT),
        small[5],
        grad_down.astype(FLOAT),
        small[6],
        small[4, : rounds * NB].reshape(rounds, NB).astype(jnp.int32),
    )


def solution(mesh):
    rows = P(("wide", "narrow"), None)
    columns = P(None, "narrow")
    return jax.shard_map(
        per_device,
        mesh=mesh,
        in_specs=(
            rows,
            rows,
            P(),
            P(),
            columns,
            columns,
            P("narrow", None),
            P(),
            P(),
            columns,
            P("narrow"),
            P("narrow", None),
            P(),
            rows,
            P("wide", None, None),
            P("wide", None),
            rows,
            rows,
        ),
        out_specs=(
            rows,
            rows,
            rows,
            rows,
            P(),
            P(),
            columns,
            columns,
            P("narrow", None),
            P(),
            P(),
            columns,
            P("narrow"),
            P("narrow", None),
            P(),
            P(),
        ),
        check_vma=False,
    )
```

time: 607 us -> 354 us (0.58); the launches traced: 597 us -> 353 us
  waiting for transfers between devices: 352 us -> 0.01 us
  Pallas kernels: 39 us -> 318 us
  matrix products: 71.6 us -> 0 us
  blocking collectives: 59.7 us -> 0 us
  other arithmetic: 45.5 us -> 10.4 us
  between operations: 14.8 us -> 0.89 us
  local copies, waits for them, and re-layouts: 13.4 us -> 21.6 us
    pallas_call x2 -> x7, Pallas kernels: 39 us -> 318 us  [the longest x5 279 us: call(): pl.pallas_call(kernel, out_shape=[jax.ShapeDtypeStruct(*o) for o in outs]...]
    psum x1 -> x0, waiting for transfers between devices: 162 us -> none  [per_device(): lax.psum((grad_query_weights.astype(HALF), grad_value_weights.astype(HALF...]
    reduce_scatter x4 -> x0, waiting for transfers between devices: 104 us -> none  [the longest x1 38.1 us: per_device(): scatter(times_transpose(grad_hidden, up_proj).astype(HALF)).astype(FLOAT)]
    all_gather x4 -> x0, waiting for transfers between devices: 85.3 us -> none  [the longest x1 28 us: per_device(): gathered_two = gather(normed_two)]
    dot_general x16 -> x0, matrix products: 71.6 us -> none  [the longest x5 22.7 us: times_transpose(): lax.dot_general(left, right, (((1,), (1,)), ((), ())), preferred_element_...]
    psum x2 -> x0, blocking collectives: 59.7 us -> none  [the longest x1 39.8 us: per_device(): lax.psum((jnp.sum(grad_normed_one * scaled_one, axis=0), jnp.sum(grad_nor...]
    reduce_sum x12 -> x0, other arithmetic: 18.7 us -> none  [the longest x1 4.63 us: per_device(): jnp.sum(by_head * by_head, axis=-1, keepdims=True) + 1e-06]
    convert_element_type x14 -> x5, other arithmetic: 23.9 us -> 9.72 us  [the longest x1 2.68 us: per_device(): grad_weights[:, heads:].astype(FLOAT)]
  transfers between devices with their start and end apart: 9 -> 2, of which waited for: 8 -> 0; matrix products, arithmetic and copies ran while one was open for 10% -> 0% of each run, Pallas kernels for 0% -> 11%
where the time goes in v2:
time: 354 us; the launch traced here: 353 us
  Pallas kernels  318 us (90%)
  local copies, waits for them, and re-layouts  21.6 us (6%)
  other arithmetic  10.4 us (3%)
    pallas_call x5, Pallas kernels, call(): pl.pallas_call(kernel, out_shape=[jax.ShapeDtypeStruct(*o) for o in outs]...  279 us
    pallas_call x1, Pallas kernels, run_attention_back(): pl.pallas_call(partial(attention_backward, rounds, width // HD, steps), g...  22.1 us
    pallas_call x1, Pallas kernels, run_attention(): pl.pallas_call(partial(attention_forward, rounds, width // HD, steps), gr...  17 us
    unnamed x57, local copies, waits for them, and re-layouts  16.1 us
  transfers between devices with their start and end apart: 2, of which 0 were waited for; matrix products, arithmetic and copies ran while one was open for 0% of the time, Pallas kernels for 11%

profile of v2, /device:TPU:0, one launch (start us, length us, event | category | flops | bytes accessed | tf_op | source)
XLA Modules:
  0.0 353.1 jit_solution(2364439160417150279)
XLA Ops:
  0.7 1.6 copy.34.buckets
  2.3 27.1 %project_in.1 = (bf16[1536,1024]{1,0:T(8,128)(2,1)}, bf16[1536,256]{1,0:T(8,128)(2,1)}, bf16[1536,256]{1,0:T(8,128)(2,1)}, bf16[1536,256]{1,0:T(8,128)(2,1)}, bf...) custom-call(bf16[384,1024]{1,0:T(8,128)(2,1)} %second_rows.1, f32[1,1024]{1,0:T(1,128)} %bitcast.49, ...), custom_call_target="tpu_custom_call" | custom-call | flops 1610612736 | bytes 10485760 | tf_op jit(solution)/shard_map/project_in/pallas_call | solution.py:229
  29.4 0.9 collective-permute-start
  31.3 1.1 copy-done.3
  32.4 1.1 copy-done.5
  33.5 1.1 copy-done.7
  34.7 1.0 copy-done.9
  35.7 1.0 copy-done.11
  36.6 17.0 %attention_forward.1 = (bf16[1536,256]{1,0:T(8,128)(2,1)S(1)}, f32[1536,128]{1,0:T(8,128)S(1)}) custom-call(s32[8]{0:T(128)S(1)} %bitcast.30, bf16[1536,256]{1,0:T(8,128)(2,1)S(1)} %copy-done.3, bf16[1536,256]{1,0:T(8,128)(2,1)S(1)} %copy-done.5, bf16[1536,256]{1,0:T(8,128)(2,1)S(1)} %copy-done.7, bf16[128,1536]{1,0:T(8,128)(2,1)S(1)} %copy-done.9, ...), custom_call_target="tpu_custom_call" | custom-call | flops 6000000000 | bytes 6291456 | tf_op jit(solution)/shard_map/attention_forward/pallas_call | solution.py:469
  53.7 0.9 copy-done.13
  54.6 0.9 copy-done.25
  55.4 52.7 %feed_in.1 = (bf16[384,1024]{1,0:T(8,128)(2,1)}, f32[384,1024]{1,0:T(8,128)}, bf16[1536,1024]{1,0:T(8,128)(2,1)}, bf16[1536,1024]{1,0:T(8,128)(2,1)}, bf16[1536,...) custom-call(bf16[1536,256]{1,0:T(8,128)(2,1)} %copy-done.13, bf16[256,1024]{1,0:T(8,128)(2,1)} %wo_any.1, ...), custom_call_target="tpu_custom_call" | custom-call | flops 6442450944 | bytes 25165824 | tf_op jit(solution)/shard_map/feed_in/pallas_call | solution.py:229
  108.2 48.7 %feed_back.1 = (bf16[384,1024]{1,0:T(8,128)(2,1)}, bf16[1536,256]{1,0:T(8,128)(2,1)}, bf16[1024,1024]{1,0:T(8,128)(2,1)}, bf16[1024,1024]{1,0:T(8,128)(2,1)}, bf...) custom-call(bf16[1536,1024]{1,0:T(8,128)(2,1)} %get-tuple-element.61.grad_hi, ...), custom_call_target="tpu_custom_call" | custom-call | flops 12884901888 | bytes 31457280 | tf_op jit(solution)/shard_map/feed_back/pallas_call | solution.py:229
  156.9 1.3 collective-permute-start.1
  158.2 0.8 fusion.3
  159.1 1.1 copy-done.15
  160.2 22.1 %attention_backward.1 = (bf16[1536,256]{1,0:T(8,128)(2,1)S(1)}, bf16[1536,256]{1,0:T(8,128)(2,1)S(1)}) custom-call(s32[8]{0:T(128)S(1)} %bitcast.31, bf16[1536,256]{1,0:T(8,128)(2,1)S(1)} %copy-done.4, bf16[1536,256]{1,0:T(8,128)(2,1)S(1)} %copy-done.15, bf16[1536,256]{1,0:T(8,128)(2,1)S(1)} %copy-done.14, ...), custom_call_target="tpu_custom_call" | custom-call | flops 10000000000 | bytes 8388608 | tf_op jit(solution)/shard_map/attention_backward/pallas_call | solution.py:581
  182.3 0.9 copy-done.1
  183.2 0.9 copy-done.2
  184.1 0.9 copy-done.24
  185.0 27.1 %project_back.1 = (bf16[384,1024]{1,0:T(8,128)(2,1)}, bf16[384,1024]{1,0:T(8,128)(2,1)}, bf16[1024,512]{1,0:T(8,128)(2,1)}, f32[8,1024]{1,0:T(8,128)}) custom-call(bf16[1536,256]{1,0:T(8,128)(2,1)} %copy-done.1, bf16[1536,256]{1,0:T(8,128)(2,1)} %copy-done.2, bf16[1024,256]{1,0:T(8,128)(2,1)} %wq.1, bf16[1024,256]{1,0:T(8,128)(2,1)} %wv.1, ...), custom_call_target="tpu_custom_call" | custom-call | flops 3221225472 | bytes 14680064 | tf_op jit(solution)/shard_map/project_back/pallas_call | solution.py:229
  212.1 0.8 slice.39
  214.2 123.3 %sum_wide.1 = (bf16[16,64,1024]{2,1,0:T(8,128)(2,1)}, bf16[16,64,1024]{2,1,0:T(8,128)(2,1)}, bf16[16,16,1024]{2,1,0:T(8,128)(2,1)}, bf16[16,64,512]{2,1,0:T(8,128)(2,1)}, f32[8,1024]{1,0:T(8,128)}) custom-call(bf16[16,64,1024]{2,1,0:T(8,128)(2,1)} %bitcast.32, bf16[16,64,1024]{2,1,0:T(8,128)(2,1)} %bitcast.33, bf16[16,16,1024]{2,1,0:T(8,128)(2,1)} %bitcast.36, ...), custom_call_target="tpu_custom_call" | custom-call | flops 1000000 | bytes 25165824 | tf_op jit(solution)/shard_map/sum_wide/pallas_call | solution.py:229
  337.5 1.7 fusion.2
  339.9 2.7 slice_convert_fusion
  342.6 1.1 bitcast_convert_fusion.2
  343.7 2.6 bitcast_convert_fusion.1
  346.3 2.6 bitcast_convert_fusion
  349.6 0.9 copy.39
  350.5 0.9 copy.40
  351.4 0.9 copy.41
  352.2 0.9 copy.42
  (54 shorter events, 3.7 us)
Async XLA Ops:
  0.6 30.6 %copy-start = (s32[1,8]{1,0:T(1,128)S(1)}, s32[1,8]{1,0:T(1,128)}, u32[]{:S(2)}) copy-start(s32[1,8]{1,0:T(1,128)} %param.33) | copy-start | bytes 100
  0.7 28.7 %copy-start.23 = (bf16[384,1024]{1,0:T(8,128)(2,1)S(1)}, bf16[384,1024]{1,0:T(8,128)(2,1)}, u32[]{:S(2)}) copy-start(bf16[384,1024]{1,0:T(8,128)(2,1)} %cotan_two.1) | copy-start | bytes 2359300
  29.4 25.2 %collective-permute-start = (bf16[384,1024]{1,0:T(8,128)(2,1)S(1)}, bf16[384,1024]{1,0:T(8,128)(2,1)S(1)}, u32[]{:S(2)}, u32[]{:S(2)}) collective-permute-start(bf16[384,1024]{1,0:T(8,128)(2,1)S(1)} %copy-done.23), channel_id=1, source_target_pairs={{0,2},{1,3},{2,0},{3,1},{4,6},{5,7},{6,4},{7,5},{8,10},{9,11},{10,... | collective-permute-start | bytes 2359304 | tf_op jit(solution)/shard_map/ppermute | solution.py:1190
  31.3 1.1 copy-start.3
  32.4 1.1 copy-start.5
  33.5 1.1 copy-start.7
  34.7 1.0 copy-start.9
  35.7 1.0 copy-start.11
  53.7 0.9 copy-start.13
  54.6 0.9 copy-start.25
  108.1 50.9 %copy-start.4 = (bf16[1536,256]{1,0:T(8,128)(2,1)S(1)}, bf16[1536,256]{1,0:T(8,128)(2,1)}, u32[]{:S(2)}) copy-start(bf16[1536,256]{1,0:T(8,128)(2,1)} %get-tuple-element.53.q_ref.all_q_ref) | copy-start | bytes 2359300
  108.2 50.9 %copy-start.6 = (bf16[1536,256]{1,0:T(8,128)(2,1)S(1)}, bf16[1536,256]{1,0:T(8,128)(2,1)}, u32[]{:S(2)}) copy-start(bf16[1536,256]{1,0:T(8,128)(2,1)} %get-tuple-element.54.k_ref) | copy-start | bytes 2359300
  108.2 50.9 %copy-start.8 = (bf16[1536,256]{1,0:T(8,128)(2,1)S(1)}, bf16[1536,256]{1,0:T(8,128)(2,1)}, u32[]{:S(2)}) copy-start(bf16[1536,256]{1,0:T(8,128)(2,1)} %get-tuple-element.55.v_ref) | copy-start | bytes 2359300
  108.2 50.9 %copy-start.10 = (bf16[128,1536]{1,0:T(8,128)(2,1)S(1)}, bf16[128,1536]{1,0:T(8,128)(2,1)}, u32[]{:S(2)}) copy-start(bf16[128,1536]{1,0:T(8,128)(2,1)} %get-tuple-element.56.fq_ref) | copy-start | bytes 1179652
  108.2 50.9 %copy-start.12 = (bf16[128,1536]{1,0:T(8,128)(2,1)S(1)}, bf16[128,1536]{1,0:T(8,128)(2,1)}, u32[]{:S(2)}) copy-start(bf16[128,1536]{1,0:T(8,128)(2,1)} %get-tuple-element.57.fk_ref) | copy-start | bytes 1179652
  108.2 50.9 %copy-start.14 = (bf16[1536,256]{1,0:T(8,128)(2,1)S(1)}, bf16[1536,256]{1,0:T(8,128)(2,1)}, u32[]{:S(2)}) copy-start(bf16[1536,256]{1,0:T(8,128)(2,1)} %copy-done.13) | copy-start | bytes 2359300
  156.9 27.2 %collective-permute-start.1 = (bf16[384,1024]{1,0:T(8,128)(2,1)}, bf16[384,1024]{1,0:T(8,128)(2,1)S(1)}, u32[]{:S(2)}, u32[]{:S(2)}) collective-permute-start(bf16[384,1024]{1,0:T(8,128)(2,1)} %get-tuple-element.72), channel_id=1, source_target_pairs={{0,2},{1,3},{2,0},{3,1},{4,6},{5,7},{6,4},{7,5},{8,10},{9,11},{10,... | collective-permute-start | bytes 2359304 | tf_op jit(solution)/shard_map/ppermute | solution.py:1198
  159.1 1.1 copy-start.15
  182.3 0.9 copy-start.1
  183.2 0.9 copy-start.2
  184.1 0.9 copy-start.24
  337.4 5.1 %copy-start.22 = (bf16[16,16,1024]{2,1,0:T(8,128)(2,1)S(1)}, bf16[16,16,1024]{2,1,0:T(8,128)(2,1)}, u32[]{:S(2)}) copy-start(bf16[16,16,1024]{2,1,0:T(8,128)(2,1)} %get-tuple-element.85) | copy-start | bytes 1572868
  337.5 6.2 %copy-start.17 = (bf16[16,64,1024]{2,1,0:T(8,128)(2,1)S(1)}, bf16[16,64,1024]{2,1,0:T(8,128)(2,1)}, u32[]{:S(2)}) copy-start(bf16[16,64,1024]{2,1,0:T(8,128)(2,1)} %get-tuple-element.86) | copy-start | bytes 6291460
  343.7 2.6 copy-start.16
  346.3 3.3 copy-start.18
  346.3 4.2 %copy-start.21 = (bf16[384,1024]{1,0:T(8,128)(2,1)S(1)}, bf16[384,1024]{1,0:T(8,128)(2,1)}, u32[]{:S(2)}) copy-start(bf16[384,1024]{1,0:T(8,128)(2,1)} %get-tuple-element.117) | copy-start | bytes 2359300
  348.9 2.4 copy-start.19
  348.9 3.3 copy-start.20

commit v3 on v0

v3 whole, which is shorter than its diff:
```python
import math
from types import SimpleNamespace

import jax
import jax.numpy as jnp
from jax import lax
from jax.experimental import pallas as pl
from jax.experimental.pallas import tpu as pltpu
from jax.sharding import PartitionSpec as P

HD = 128
GROUP = 64
NB = 24
MOST = 768
BLOCK = 256
LANES = 128
CHUNK = 128
NARROW = 4
VMEM_LIMIT = 60 << 20

FLOAT = jnp.float32
HALF = jnp.bfloat16
NEG = -1e30
EXP_SCALE = math.log2(math.e) / math.sqrt(HD)
FACTOR = 1.0 / math.sqrt(HD)
MESH = pl.DeviceIdType.MESH
IN_VMEM = pl.BlockSpec(memory_space=pltpu.VMEM)
IN_SMEM = pl.BlockSpec(memory_space=pltpu.SMEM)
ANYWHERE = pl.BlockSpec(memory_space=pl.ANY)
DMA = pltpu.SemaphoreType.DMA
WIDE = "wide"
DOCS = "docs"
FROM_HBM = "_any"


def normalize(inputs):
    center = inputs - jnp.mean(inputs, axis=-1, keepdims=True)
    inverse = lax.rsqrt(jnp.mean(center * center, axis=-1, keepdims=True) + 1e-05)
    return (center * inverse, inverse)


def norm_back(grad_out, scaled, inverse, gain):
    spread = grad_out * gain
    return inverse * (
        spread
        - jnp.mean(spread, axis=-1, keepdims=True)
        - scaled * jnp.mean(spread * scaled, axis=-1, keepdims=True)
    )


def contract_rows(left, right):
    return lax.dot_general(left, right, (((0,), (0,)), ((), ())), preferred_element_type=FLOAT)


def times_transpose(left, right):
    return lax.dot_general(left, right, (((1,), (1,)), ((), ())), preferred_element_type=FLOAT)


def times(left, right):
    return jnp.dot(left, right, preferred_element_type=FLOAT)


def column_sums(rows):
    return times(jnp.ones((8, rows.shape[0]), rows.dtype), rows)[0:1]


class Place:
    def __init__(self):
        index = lax.axis_index("narrow")
        core, chip = lax.rem(index, 2), lax.div(index, 2)
        self.me = index
        self.near = 2 * chip + 1 - core
        self.far = 2 * (1 - chip) + core
        self.cross = 2 * (1 - chip) + 1 - core


def span(start, size):
    return pl.ds(pl.multiple_of(start, size), size)


def remote(source, target, sent, arrived, other):
    return pltpu.make_async_remote_copy(
        src_ref=source,
        dst_ref=target,
        send_sem=sent,
        recv_sem=arrived,
        device_id={"narrow": other},
        device_id_type=MESH,
    )


class Gather:
    def __init__(self, place, whole, rows, sems):
        self.place, self.whole, self.rows = place, whole, rows
        self.sent, self.arrived = sems
        self.chunks = rows // CHUNK

    def at(self, owner, chunk):
        return self.whole.at[span(owner * self.rows + chunk * CHUNK, CHUNK), :]

    def copy(self, lane, owner, chunk, other):
        index = lane * self.chunks + chunk
        piece = self.at(owner, chunk)
        return remote(piece, piece, self.sent.at[index], self.arrived.at[index], other)

    def to_far(self, chunk):
        return self.copy(0, self.place.me, chunk, self.place.far)

    def to_near(self, chunk):
        return self.copy(1, self.place.me, chunk, self.place.near)

    def onward(self, chunk):
        return self.copy(2, self.place.far, chunk, self.place.near)

    def send(self, chunk):
        self.to_far(chunk).start()
        self.to_near(chunk).start()

    def take_near(self, chunk):
        self.to_near(chunk).wait_recv()

    def take_far(self, chunk):
        self.to_far(chunk).wait_recv()
        self.onward(chunk).start()

    def take_cross(self, chunk):
        self.onward(chunk).wait_recv()

    def finish(self):
        @pl.loop(0, self.chunks)
        def _(chunk):
            self.to_far(chunk).wait_send()
            self.to_near(chunk).wait_send()
            self.onward(chunk).wait_send()


class Scatter:
    def __init__(self, place, term, rows, buffers, sems):
        self.place, self.term, self.rows = place, term, rows
        self.near_out, self.near_in, self.far_out, self.far_in = buffers
        self.sent, self.arrived = sems
        self.chunks = rows // CHUNK

    def to_near(self, part, chunk):
        index = part * self.chunks + chunk
        at = span(chunk * CHUNK, CHUNK)
        return remote(
            self.near_out.at[part, at, :],
            self.near_in.at[part, at, :],
            self.sent.at[index],
            self.arrived.at[index],
            self.place.near,
        )

    def to_far(self, chunk):
        index = 2 * self.chunks + chunk
        at = span(chunk * CHUNK, CHUNK)
        return remote(
            self.far_out.at[at, :], self.far_in.at[at, :], self.sent.at[index], self.arrived.at[index], self.place.far
        )

    def part(self, owner, chunk):
        return self.term(span(owner * self.rows + chunk * CHUNK, CHUNK))

    def start(self, between=lambda: None):
        @pl.loop(0, self.chunks)
        def _(chunk):
            self.near_out[0, span(chunk * CHUNK, CHUNK), :] = self.part(self.place.cross, chunk).astype(HALF)
            self.to_near(0, chunk).start()

        between()

        @pl.loop(0, self.chunks)
        def _(chunk):
            at = span(chunk * CHUNK, CHUNK)
            own = self.part(self.place.far, chunk)
            self.to_near(0, chunk).wait_recv()
            self.far_out[at, :] = (own + self.near_in[0, at, :].astype(FLOAT)).astype(HALF)
            self.to_far(chunk).start()

        between()

        @pl.loop(0, self.chunks)
        def _(chunk):
            self.near_out[1, span(chunk * CHUNK, CHUNK), :] = self.part(self.place.near, chunk).astype(HALF)
            self.to_near(1, chunk).start()

    def chip_sum(self, chunk):
        own = self.part(self.place.me, chunk)
        self.to_near(1, chunk).wait_recv()
        return own + self.near_in[1, span(chunk * CHUNK, CHUNK), :].astype(FLOAT)

    def take_far(self, chunk):
        self.to_far(chunk).wait_recv()
        return self.far_in[span(chunk * CHUNK, CHUNK), :].astype(FLOAT)

    def finish(self):
        @pl.loop(0, self.chunks)
        def _(chunk):
            self.to_near(0, chunk).wait_send()
            self.to_near(1, chunk).wait_send()
            self.to_far(chunk).wait_send()


def pair_features(orders, docs, query_features, key_features, found):
    rounds, length = orders.shape
    groups = length // GROUP
    high_count = length // LANES
    high_rows = -(-high_count // 8) * 8
    count = docs.shape[0]
    depth = query_features.shape[0]
    lane = lax.broadcasted_iota(jnp.int32, (LANES, length), 1)
    low_at = lax.broadcasted_iota(jnp.int32, (LANES, length), 0)
    high_at = lax.broadcasted_iota(jnp.int32, (high_rows, length), 0)
    group_at = lax.broadcasted_iota(jnp.int32, (groups, LANES), 0).astype(FLOAT)
    sorted_group = lax.shift_right_logical(lane, int(math.log2(GROUP))).astype(FLOAT)

    @pl.loop(0, rounds)
    def _(index):
        row = orders[pl.ds(index, 1), :]
        high = jnp.where(high_at == lax.shift_right_logical(row, int(math.log2(LANES))), 1.0, 0.0)
        low = jnp.where(low_at == (row & (LANES - 1)), sorted_group, 0.0)
        found[index, :high_rows, :LANES] = times_transpose(high.astype(HALF), low.astype(HALF))
    place = lax.broadcasted_iota(jnp.int32, (count, LANES), 1)
    which = lax.broadcasted_iota(jnp.int32, (count, LANES), 0)
    begins = jnp.zeros((count, LANES), jnp.int32)
    ends = jnp.zeros((count, LANES), jnp.int32)
    begin = jnp.int32(0)
    for doc in range(count):
        end = begin + docs[doc]
        begins = jnp.where(which == doc, begin, begins)
        ends = jnp.where(which == doc, end, ends)
        begin = end
    rest = jnp.zeros((depth - rounds * groups - count, LANES), FLOAT)
    for block in range(high_count):
        mine, window = [], []
        for index in range(rounds):
            own = found[index, block : block + 1, :LANES]
            after = jnp.where(own == groups - 1.0, 0.0, own + 1.0)
            here = group_at == own
            mine.append(jnp.where(here, 1.0, 0.0))
            window.append(jnp.where(here | (group_at == after), 1.0, 0.0))
        at = place + block * LANES
        same = jnp.where((at >= begins) & (at < ends), 1.0, 0.0)
        lanes = slice(block * LANES, (block + 1) * LANES)
        query_features[:, lanes] = jnp.concatenate([*mine, same * (2.0 * rounds), rest], axis=0).astype(HALF)
        key_features[:, lanes] = jnp.concatenate([*window, same, rest], axis=0).astype(HALF)


def in_turn(place, step):
    flip_core, flip_chip = lax.rem(step, 2), lax.div(step, 2)
    core, chip = lax.rem(place.me, 2), lax.div(place.me, 2)
    core = core + flip_core * (1 - 2 * core)
    chip = chip + flip_chip * (1 - 2 * chip)
    return 2 * chip + core


def take_in_turn(gather, step):
    takes = (gather.take_near, gather.take_far, gather.take_cross)

    @pl.loop(0, gather.chunks)
    def _(chunk):
        for index, take in enumerate(takes):
            if isinstance(step, int):
                if step == index + 1:
                    take(chunk)
            else:
                pl.when(step == index + 1)(lambda take=take: take(chunk))


def pair_bias(query_features, key_features, rounds, diagonal):
    counts = jnp.maximum(contract_rows(key_features, query_features) - 2.0 * rounds, 0.0)
    bias = jnp.where(counts > 0.0, jnp.log2(counts), NEG)
    if diagonal:
        key_at = lax.broadcasted_iota(jnp.int32, bias.shape, 0)
        query_at = lax.broadcasted_iota(jnp.int32, bias.shape, 1)
        bias = jnp.where(key_at < query_at, bias, NEG)
    return bias


def band_steps(length):
    return min(-(-(MOST - 1) // BLOCK), length // BLOCK - 1) + 1


def block_biases(block, steps, features, rounds, bias):
    query_features, key_features = features
    at = span(block * BLOCK, BLOCK)
    for step in range(steps):
        bias[step] = pair_bias(
            query_features[:, at], key_features[:, span((block - step) * BLOCK, BLOCK)], rounds, step == 0
        )


def attend(block, steps, rounds, queries, keys, values, features, merged, logs, bias, scores):
    at = span(block * BLOCK, BLOCK)
    heads = queries.shape[1] // HD
    block_biases(block, steps, features, rounds, bias)
    for head in range(heads):
        part = slice(head * HD, (head + 1) * HD)
        query = queries[at, part]
        peak = jnp.full((1, BLOCK), 2 * NEG, FLOAT)
        for step in range(steps):
            key_at = span((block - step) * BLOCK, BLOCK)
            score = times_transpose(keys[key_at, part], query) * EXP_SCALE + bias[step]
            scores[span((head * steps + step) * BLOCK, BLOCK), :] = score
            peak = jnp.maximum(peak, jnp.max(score, axis=0, keepdims=True))
        alone = peak < 0.5 * NEG
        peak = jnp.where(alone, 0.0, peak)
        total = jnp.zeros((1, BLOCK), FLOAT)
        mixed = jnp.zeros((HD, BLOCK), FLOAT)
        for step in range(steps):
            key_at = span((block - step) * BLOCK, BLOCK)
            powers = jnp.exp2(scores[span((head * steps + step) * BLOCK, BLOCK), :] - peak)
            total = total + jnp.sum(powers, axis=0, keepdims=True)
            mixed = mixed + contract_rows(values[key_at, part], powers.astype(HALF))
        total = jnp.where(alone, 1.0, total)
        mixed = jnp.where(alone, values[at, part].astype(FLOAT).T, mixed / total)
        merged[at, part] = mixed.T.astype(HALF)
        logs[head : head + 1, at] = jnp.where(alone, -NEG, peak + jnp.log2(total))


def attend_back(block, steps, rounds, queries, keys, values, features, grads, merged, logs, dq, dk, dv, bias, after):
    at = span(block * BLOCK, BLOCK)
    heads = queries.shape[1] // HD
    block_biases(block, steps, features, rounds, bias)
    ones = jnp.ones((8, HD), HALF)
    for head in range(heads):
        part = slice(head * HD, (head + 1) * HD)
        query, grad = queries[at, part], grads[at, part]
        log_sum = logs[head : head + 1, at]
        product = grad.astype(FLOAT) * merged[at, part].astype(FLOAT)
        coarse = product.astype(HALF)
        fine = (product - coarse.astype(FLOAT)).astype(HALF)
        along = (times_transpose(ones, coarse) + times_transpose(ones, fine))[0:1]
        grad_query = jnp.zeros((HD, BLOCK), FLOAT)
        for step in range(steps):
            key_at = span((block - step) * BLOCK, BLOCK)
            key = keys[key_at, part]
            weights = jnp.exp2(times_transpose(key, query) * EXP_SCALE + bias[step] - log_sum)
            grad_probs = times_transpose(values[key_at, part], grad)
            grad_scores = (weights * (grad_probs - along)).astype(HALF)
            grad_value = times(weights.astype(HALF), grad)
            grad_key = times(grad_scores, query)
            if step == 0:
                dv[key_at, part] = grad_value
                dk[key_at, part] = grad_key
            else:
                dv[key_at, part] += grad_value
                dk[key_at, part] += grad_key
            grad_query = grad_query + contract_rows(key, grad_scores)
        dq[at, part] = grad_query.T
        after(head)


def finish_attention(queries, grads, logs, dq, dk, dv, grad_query, grad_value):
    length, width = queries.shape

    @pl.loop(0, length // BLOCK)
    def _(block):
        at = span(block * BLOCK, BLOCK)
        alone = jnp.where(logs[:, at] == -NEG, 1.0, 0.0).T
        for head in range(width // HD):
            part = slice(head * HD, (head + 1) * HD)
            grad_value[at, part] = (dv[at, part] + alone[:, head : head + 1] * grads[at, part].astype(FLOAT)).astype(HALF)
            query = queries[at, part].astype(FLOAT)
            key_scale = lax.rsqrt(jnp.sum(query * query, axis=-1, keepdims=True) + 1e-06)
            unit = query * key_scale
            grad_key = dk[at, part] * FACTOR
            key_along = jnp.sum(grad_key * unit, axis=-1, keepdims=True)
            grad_query[at, part] = (dq[at, part] * FACTOR + key_scale * (grad_key - unit * key_along)).astype(HALF)


def gelu_and_slope(hidden):
    square = hidden * hidden
    bend = jnp.tanh(math.sqrt(2.0 / math.pi) * hidden * (1.0 + 0.044715 * square))
    half_more = 0.5 + 0.5 * bend
    slope = half_more + 0.5 * hidden * (1.0 - bend * bend) * (
        math.sqrt(2.0 / math.pi) * (1.0 + 3.0 * 0.044715 * square)
    )
    return hidden * half_more, slope


def weight_grad(result, left, right, rows=None, add=False):
    width = 256
    height = result.shape[1] * result.shape[2] // right.shape[1]
    pieces = width // height
    rows = slice(None) if rows is None else rows

    @pl.loop(0, left.shape[1] // width)
    def _(index):
        block = contract_rows(left[rows, span(index * width, width)], right[rows, :])
        at = pl.ds(index * pieces, pieces)
        block = block.reshape(pieces, *result.shape[1:])
        if add:
            block = block + result[at].astype(FLOAT)
        result[at] = block.astype(result.dtype)


def ring_place(members, index):
    column, row = lax.rem(index, 2), lax.div(index, 2)
    return row + column * (members - 1 - 2 * row)


def ring_member(members, place):
    back = lax.div(place, members // 2)
    return 2 * place + back * (2 * (members - 1 - place) + 1 - 2 * place)


class Ring:
    def __init__(self, members, data, landed, result, sent, arrived, kept):
        self.members, self.data, self.landed, self.result = members, data, landed, result
        self.sent, self.arrived, self.kept, self.stage = sent, arrived, kept, 0
        self.here = ring_place(members, lax.axis_index("wide"))
        self.neighbours = (
            ring_member(members, lax.rem(self.here + 1, members)),
            ring_member(members, lax.rem(self.here + members - 1, members)),
        )

    def piece(self, direction, step):
        if direction == 0:
            return 2 * lax.rem(self.here - step + 2 * self.members, self.members)
        return 2 * lax.rem(self.here + step, self.members) + 1

    def copy(self, direction, step, at, gathering, fresh):
        index = direction * 2 * (self.members - 1) + step
        source = self.landed if gathering and not fresh else self.data
        return pltpu.make_async_remote_copy(
            src_ref=source.at[at],
            dst_ref=self.landed.at[at],
            send_sem=self.sent.at[index],
            recv_sem=self.arrived.at[index],
            device_id={"wide": self.neighbours[direction]},
            device_id_type=MESH,
        )

    def outgoing(self, direction, step, gathering=False, fresh=False):
        return self.copy(direction, step, self.piece(direction, step), gathering, fresh)

    def incoming(self, direction, step, gathering=False):
        return self.copy(direction, step, self.piece(direction, step + 1), gathering, False)

    def begin(self):
        for direction in range(2):
            self.outgoing(direction, 0).start()

    def add(self, direction, step):
        self.incoming(direction, step).wait_recv()
        at = self.piece(direction, step + 1)
        self.data[at] = (self.data[at].astype(FLOAT) + self.landed[at].astype(FLOAT)).astype(HALF)
        return at

    def keep(self, direction, step):
        at = self.piece(direction, step)
        source = self.data if isinstance(step, int) and step == self.members - 1 else self.landed
        return pltpu.make_async_copy(
            source.at[at], self.result.at[at], self.kept.at[direction * self.members + step - (self.members - 1)]
        )

    def advance(self):
        stage, last = self.stage, self.members - 1
        if stage == 14:
            return
        self.stage = stage + 1
        low, high = stage * 2 * last // 14, (stage + 1) * 2 * last // 14

        def repeat(begin, end, act):
            if end == begin + 1:
                act(begin)
            elif end > begin:
                pl.loop(begin, end)(act)

        def reduce(step):
            for direction in range(2):
                self.add(direction, step)
                self.outgoing(direction, step + 1).start()

        def forward(step):
            for direction in range(2):
                self.incoming(direction, step, True).wait_recv()
                self.outgoing(direction, step + 1, True).start()
                self.keep(direction, step + 1).start()

        repeat(low, min(high, last - 1), reduce)
        if low <= last - 1 < high:
            for direction in range(2):
                self.add(direction, last - 1)
                self.outgoing(direction, last, True, True).start()
                self.keep(direction, last).start()
        repeat(max(low, last), min(high, 2 * last - 1), forward)
        if low <= 2 * last - 1 < high:
            for direction in range(2):
                self.incoming(direction, 2 * last - 1, True).wait_recv()
                self.keep(direction, 2 * last).start()

    def finish(self):
        last = self.members - 1
        for direction in range(2):
            self.keep(direction, last).wait()
            self.outgoing(direction, last, True, True).wait_send()

        @pl.loop(0, last)
        def _(step):
            for direction in range(2):
                self.outgoing(direction, step).wait_send()

        @pl.loop(last + 1, 2 * last)
        def _(step):
            for direction in range(2):
                self.outgoing(direction, step, True).wait_send()
                self.keep(direction, step).wait()

        for direction in range(2):
            self.keep(direction, 2 * last).wait()


class Exchange:
    def __init__(self, members, data, landed, result, first, unit, bits, sems, stored):
        self.members, self.data, self.landed, self.result = members, data, landed, result
        self.first, self.unit, self.bits = first, unit, bits
        self.sent, self.arrived, self.stored, self.stage = *sems, stored, 0
        self.wide = lax.axis_index("wide")

    def bit(self, step):
        return lax.rem(lax.div(self.wide, 1 << self.bits[step]), 2)

    def size(self, step):
        return self.unit * (self.members >> (step + 1))

    def part(self, step, kept):
        start = self.first
        for before in range(step):
            start = start + self.bit(before) * self.size(before)
        bit = self.bit(step)
        return pl.ds(start + (bit if kept else 1 - bit) * self.size(step), self.size(step))

    def landing(self, step):
        return pl.ds(self.first + self.unit * self.members - 2 * self.size(step), self.size(step))

    def copy(self, step, gathering):
        index = step + gathering * len(self.bits)
        at = self.part(step, gathering)
        source = self.result if gathering and step < len(self.bits) - 1 else self.data
        return pltpu.make_async_remote_copy(
            src_ref=source.at[at],
            dst_ref=self.result.at[at] if gathering else self.landed.at[self.landing(step)],
            send_sem=self.sent.at[index],
            recv_sem=self.arrived.at[index],
            device_id={"wide": self.wide + (1 - 2 * self.bit(step)) * (1 << self.bits[step])},
            device_id_type=MESH,
        )

    def begin(self):
        self.copy(0, False).start()

    def advance(self):
        count, stage = len(self.bits), self.stage
        if stage == 2 * count:
            return
        self.stage = stage + 1
        if stage < count:
            self.copy(stage, False).wait_recv()
            kept, landed = self.part(stage, True), self.landing(stage)

            @pl.loop(0, self.size(stage))
            def _(index):
                at = kept.start + index
                self.data[at] = (
                    self.data[at].astype(FLOAT) + self.landed[landed.start + index].astype(FLOAT)
                ).astype(HALF)

        else:
            self.copy(2 * count - 1 - stage, True).wait_recv()
        if stage < count - 1:
            self.copy(stage + 1, False).start()
            return
        if stage == count - 1:
            self.store().start()
        if stage == count:
            self.store().wait()
        if stage < 2 * count - 1:
            self.copy(2 * count - 2 - stage, True).start()

    def store(self):
        at = self.part(len(self.bits) - 1, True)
        return pltpu.make_async_copy(self.data.at[at], self.result.at[at], self.stored)

    def finish(self):
        for step in range(len(self.bits)):
            self.copy(step, False).wait_send()
            self.copy(step, True).wait_send()


class Everyone:
    def __init__(self, axis, slots, sent, arrived):
        self.axis, self.slots, self.sent, self.arrived = axis, slots, sent, arrived
        self.me, self.members = lax.axis_index(axis), slots.shape[0]

    def copy(self, step):
        mine = self.slots.at[self.me]
        return pltpu.make_async_remote_copy(
            src_ref=mine,
            dst_ref=mine,
            send_sem=self.sent.at[step],
            recv_sem=self.arrived.at[step],
            device_id={self.axis: lax.rem(self.me + step, self.members)},
            device_id_type=MESH,
        )

    def send(self, value):
        self.slots[self.me] = value

        @pl.loop(1, self.members)
        def _(step):
            self.copy(step).start()

    def total(self):
        @pl.loop(1, self.members)
        def _(step):
            self.copy(step).wait()

        return lax.fori_loop(1, self.members, lambda index, total: total + self.slots[index], self.slots[0])


def advance(*exchanges):
    for exchange in exchanges:
        exchange.advance()


def meet_all(members):
    barrier = pltpu.get_barrier_semaphore()
    narrow, wide = lax.axis_index("narrow"), lax.axis_index("wide")

    @pl.loop(1, NARROW)
    def _(step):
        pl.semaphore_signal(
            barrier, inc=1, device_id={"narrow": lax.rem(narrow + step, NARROW)}, device_id_type=MESH
        )

    @pl.loop(1, members)
    def _(step):
        pl.semaphore_signal(barrier, inc=1, device_id={"wide": lax.rem(wide + step, members)}, device_id_type=MESH)

    pl.semaphore_wait(barrier, NARROW - 1 + members - 1)


def layer(members, ref):
    place = Place()
    second_rows = ref.stream_two
    rows, width = second_rows.shape
    orders, docs = ref.orders, ref.docs
    rounds, length = orders.shape
    heads = ref.wq.shape[1]
    chunks = rows // CHUNK
    whole_one, whole_two, cotans, grad_rows = (ref.whole_one, ref.whole_two, ref.cotans, ref.grad_rows)
    queries, keys, values, merged, logs = (ref.queries, ref.keys, ref.values, ref.merged, ref.logs)
    features = (ref.query_features, ref.key_features)
    wq, wv, wo, up, down = (ref.wq, ref.wv, ref.wo, ref.up, ref.down)
    active, grad_hidden, middle, first_rows = (ref.active, ref.grad_hidden, ref.middle, ref.first_rows)
    grad_merged, bias, sums = ref.grad_merged, ref.bias, ref.sums
    dq, dk, dv = (ref.totals.at[pl.ds(i * length, length), :] for i in range(3))
    own_at, far_at = span(place.me * rows, rows), span(place.far * rows, rows)
    loads, stores = ref.loads, ref.stores

    def load(index, source, target):
        copy = pltpu.make_async_copy(source, target, loads.at[index])
        copy.start()
        return copy

    load_wq, load_wv = load(0, ref.wq_any, wq), load(1, ref.wv_any, wv)
    load_cotan = load(2, ref.cotan_two_any, cotans.at[own_at, :])
    load_wo, load_first = load(3, ref.wo_any, wo), load(4, ref.stream_one_any, first_rows)
    load_down, load_up = load(5, ref.down_any, down), load(6, ref.up_any, up)
    meet_all(members)

    up_ring, down_ring = rings = [
        Ring(
            members, ref.sum_data[i], ref.sum_landed[i], ref.sum_results[i], ref.ring_sent.at[i], ref.ring_arrived.at[i],
            ref.ring_kept.at[i],
        )
        for i in range(2)
    ]
    bits = list(range(members.bit_length() - 1))
    swapped = bits[1::-1] + bits[2:]
    lanes = ((2, 0, bits), (2, members, swapped), (3, 0, bits), (3, members, swapped))
    out_sum, out_swap, in_sum, in_swap = exchanges = [
        Exchange(
            members, ref.sum_data[array], ref.sum_landed[array], ref.sum_results[array], first, 1, order,
            (ref.sum_sent.at[lane], ref.sum_arrived.at[lane]), ref.sum_stored.at[lane],
        )
        for lane, (array, first, order) in enumerate(lanes)
    ]
    queue = [up_ring, down_ring]

    def serve(*more):
        ring = queue.pop(0)
        queue.append(ring)
        advance(ring, *more)

    gather = Gather(place, whole_one, rows, (ref.gather_sent.at[0], ref.gather_arrived.at[0]))

    @pl.loop(0, chunks)
    def _(chunk):
        scaled, _ = normalize(second_rows[span(chunk * CHUNK, CHUNK), :].astype(FLOAT))
        normed = (scaled * ref.gain_one[...] + ref.shift_one[...]).astype(HALF)
        whole_one[span(place.me * rows + chunk * CHUNK, CHUNK), :] = normed
        gather.send(chunk)

    pair_features(orders, docs, *features, bias)
    level = lax.broadcasted_iota(jnp.int32, (LANES, rows), 0)
    counted = jnp.ones((8, rows), HALF)
    sums[...] = jnp.zeros_like(sums)
    for index in range(rounds):
        found = jnp.where(level == ref.buckets[index : index + 1, :], 1.0, 0.0).astype(HALF)
        sums[4:5, index * LANES : (index + 1) * LANES] = times_transpose(counted, found)[0:1]
    load_wq.wait()
    load_wv.wait()

    def project(owner):
        at = span(owner * rows, rows)
        query = times(whole_one[at, :], wq[...]).astype(HALF)
        queries[at, :] = query
        for head in range(heads // HD):
            part = query[:, head * HD : (head + 1) * HD].astype(FLOAT)
            scale = lax.rsqrt(jnp.sum(part * part, axis=-1, keepdims=True) + 1e-06)
            keys[at, head * HD : (head + 1) * HD] = (part * scale).astype(HALF)
        values[at, :] = times(whole_one[at, :], wv[...]).astype(HALF)

    @pl.loop(0, NARROW)
    def _(step):
        take_in_turn(gather, step)
        project(in_turn(place, step))

    gather.finish()

    load_cotan.wait()
    spread = Gather(place, cotans, rows, (ref.gather_sent.at[1], ref.gather_arrived.at[1]))

    @pl.loop(0, chunks)
    def _(chunk):
        spread.send(chunk)

    steps = band_steps(length)
    blocks = length // BLOCK

    def forward(block, count):
        attend(block, count, rounds, queries, keys, values, features, merged, logs, bias, ref.totals)

    for block in range(steps - 1):
        forward(block, block + 1)

    @pl.loop(steps - 1, blocks)
    def _(block):
        forward(block, steps)

    buffers = (ref.near_out, ref.near_in, ref.far_out, ref.far_in)
    load_wo.wait()
    scatter = Scatter(
        place, lambda at: times(merged[at, :], wo[...]), rows, buffers, (ref.scatter_sent.at[0], ref.scatter_arrived.at[0])
    )
    scatter.start()
    load_first.wait()

    @pl.loop(0, chunks)
    def _(chunk):
        at = span(chunk * CHUNK, CHUNK)
        middle[at, :] = first_rows[at, :].astype(FLOAT) + scatter.chip_sum(chunk)

    @pl.loop(0, chunks)
    def _(chunk):
        spread.take_near(chunk)
        spread.take_far(chunk)

    load_down.wait()
    half_width = width // 2

    def grad_active(owner):
        @pl.loop(0, 2)
        def _(half):
            at = span(half * half_width, half_width)
            grad_hidden[span(owner * rows, rows), at] = times_transpose(
                cotans[span(owner * rows, rows), :], down[at, :]
            ).astype(HALF)

    @pl.loop(0, NARROW)
    def _(step):
        @pl.when(step == NARROW - 1)
        def _():
            @pl.loop(0, chunks)
            def _(chunk):
                spread.take_cross(chunk)

        grad_active(in_turn(place, step))

    gather = Gather(place, whole_two, rows, (ref.gather_sent.at[2], ref.gather_arrived.at[2]))
    load_up.wait()

    @pl.loop(0, chunks)
    def _(chunk):
        at = span(chunk * CHUNK, CHUNK)
        value = middle[at, :] + scatter.take_far(chunk)
        middle[at, :] = value
        first_rows[at, :] = value.astype(HALF)
        scaled, _ = normalize(value)
        whole_two[span(place.me * rows + chunk * CHUNK, CHUNK), :] = (
            scaled * ref.gain_two[...] + ref.shift_two[...]
        ).astype(HALF)
        gather.send(chunk)

    store_one = pltpu.make_async_copy(first_rows, ref.out_one, stores.at[0])
    store_one.start()

    def feed(step):
        take_in_turn(gather, step)
        row_at = span(in_turn(place, step) * rows, rows)

        @pl.loop(0, 2)
        def _(half):
            at = span(half * half_width, half_width)
            value, slope = gelu_and_slope(times(whole_two[row_at, :], up[:, at]) + ref.up_bias[:, at])
            active[row_at, at] = value.astype(HALF)
            grad_hidden[row_at, at] = (grad_hidden[row_at, at].astype(FLOAT) * slope).astype(HALF)

    chip = lax.div(place.me, 2)
    here, there = span(chip * 2 * rows, 2 * rows), span((1 - chip) * 2 * rows, 2 * rows)
    pl.loop(0, NARROW // 2)(feed)
    weight_grad(ref.sum_data[1], active, cotans, here)
    weight_grad(ref.sum_data[0], whole_two, grad_hidden, here)
    pl.loop(NARROW // 2, NARROW)(feed)
    scatter.finish()

    scatter = Scatter(
        place,
        lambda at: times_transpose(grad_hidden[at, :], up[...]),
        rows,
        buffers,
        (ref.scatter_sent.at[1], ref.scatter_arrived.at[1]),
    )
    scatter.start()
    store_one.wait()
    load_cotan_one = load(7, ref.cotan_one_any, first_rows)
    weight_grad(ref.sum_data[1], active, cotans, there, True)
    down_ring.begin()
    weight_grad(ref.sum_data[0], whole_two, grad_hidden, there, True)
    up_ring.begin()
    queue.reverse()
    back = Gather(place, grad_rows, rows, (ref.gather_sent.at[3], ref.gather_arrived.at[3]))
    load_cotan_one.wait()

    for chunk in range(chunks):
        at = span(chunk * CHUNK, CHUNK)
        grad_normed = scatter.chip_sum(chunk) + scatter.take_far(chunk)
        scaled, inverse = normalize(middle[at, :])
        grad = first_rows[at, :].astype(FLOAT) + norm_back(grad_normed, scaled, inverse, ref.gain_two[...])
        grad_rows[span(place.me * rows + chunk * CHUNK, CHUNK), :] = grad.astype(HALF)
        back.send(chunk)
        sums[2:3, :] += jnp.sum(grad_normed * scaled, axis=0, keepdims=True)
        sums[3:4, :] += jnp.sum(grad_normed, axis=0, keepdims=True)
        serve()
        serve()

    def merge_back(step):
        at = span(in_turn(place, step) * rows, rows)
        grad_merged[at, :] = times_transpose(grad_rows[at, :], wo[...]).astype(HALF)

    store_grad = pltpu.make_async_copy(grad_rows.at[own_at, :], ref.grad_one, stores.at[1])
    store_grad.start()
    own_sums = ref.wide_all.at[lax.axis_index(WIDE)]
    own_sums[5:6, :] = column_sums(grad_hidden[...])
    own_sums[6:7, :] = column_sums(cotans[...])
    scatter.finish()
    gather.finish()
    spread.finish()

    serve()
    merge_back(0)
    take_in_turn(back, 1)
    merge_back(1)
    serve()
    for chunk in range(chunks):
        back.take_far(chunk)
        serve()
    merge_back(2)
    take_in_turn(back, 3)
    merge_back(3)
    serve()
    weight_grad(ref.sum_data[2], merged, grad_rows)
    out_sum.begin()
    out_swap.begin()
    serve()

    fed = Scatter(
        place, lambda at: times(active[at, :], down[...]), rows, buffers, (ref.scatter_sent.at[2], ref.scatter_arrived.at[2])
    )
    fed.start(serve)
    serve()

    for block in range(blocks):

        def after(head, block=block):
            if block > 1 or head == heads // HD - 1:
                serve(*([out_sum, out_swap][head % 2 : head % 2 + 1] if block > 1 else []))

        attend_back(
            block, min(block + 1, steps), rounds, queries, keys, values, features, grad_merged, merged, logs, dq, dk, dv, bias, after
        )

    grad_query, grad_value = ref.grad_query, ref.grad_value
    finish_attention(queries, grad_merged, logs, dq, dk, dv, grad_query, grad_value)
    serve()
    weight_grad(ref.sum_data[3], whole_one, ref.grad_both)
    in_sum.begin()
    in_swap.begin()
    serve(out_sum, out_swap)

    @pl.loop(0, chunks)
    def _(chunk):
        at = span(chunk * CHUNK, CHUNK)
        middle[at, :] = fed.chip_sum(chunk) + fed.take_far(chunk) + ref.down_bias[...]
        first_two = second_rows[at, :].astype(FLOAT) + middle[at, :]
        cotans[span(place.near * rows + chunk * CHUNK, CHUNK), :] = first_two.astype(HALF)

    store_two = pltpu.make_async_copy(cotans.at[span(place.near * rows, rows), :], ref.out_two, stores.at[2])
    store_two.start()
    fed.finish()
    ready = ref.ready
    for other in (place.near, place.far):
        pl.semaphore_signal(ready, inc=1, device_id={"narrow": other}, device_id_type=MESH)
    pl.semaphore_wait(ready, 2)

    scatter = Scatter(
        place,
        lambda at: times_transpose(grad_query[at, :], wq[...]) + times_transpose(grad_value[at, :], wv[...]),
        rows,
        buffers,
        (ref.scatter_sent.at[3], ref.scatter_arrived.at[3]),
    )
    scatter.start(lambda: serve(in_swap, in_sum))
    serve(in_swap, in_sum)

    for chunk in range(chunks):
        at = span(chunk * CHUNK, CHUNK)
        grad_normed = scatter.chip_sum(chunk) + scatter.take_far(chunk)
        scaled, inverse = normalize(second_rows[at, :].astype(FLOAT))
        mine = span(place.me * rows + chunk * CHUNK, CHUNK)
        cotans[mine, :] = (
            cotans[mine, :].astype(FLOAT) + norm_back(grad_normed, scaled, inverse, ref.gain_one[...])
        ).astype(HALF)
        sums[0:1, :] += jnp.sum(grad_normed * scaled, axis=0, keepdims=True)
        sums[1:2, :] += jnp.sum(grad_normed, axis=0, keepdims=True)
        serve(*exchanges)
        serve()

    store_last = pltpu.make_async_copy(cotans.at[own_at, :], ref.grad_two, stores.at[3])
    store_last.start()
    over_narrow = Everyone("narrow", ref.narrow_all, ref.narrow_sent, ref.narrow_arrived)
    over_wide = Everyone("wide", ref.wide_all, ref.wide_sent, ref.wide_arrived)
    over_narrow.send(sums[...])
    serve(*exchanges)
    sums[...] = over_narrow.total()
    sums[5:7, :] = own_sums[5:7, :]
    over_wide.send(sums[...])
    while min(exchange.stage for exchange in exchanges) < 2 * len(bits) or min(ring.stage for ring in rings) < 14:
        serve(*exchanges)
    ref.small[...] = over_wide.total()
    scatter.finish()
    back.finish()
    for copy in (store_grad, store_two, store_last):
        copy.wait()
    for exchange in [*exchanges, *rings]:
        exchange.finish()


def pieces(members, shape):
    columns = shape[1] if members <= 8 else LANES
    return (2 * members, shape[0] * shape[1] // (2 * members * columns), columns)


def run_layer(members, args):
    rows, width = args.stream_two.shape
    length, heads, hidden = NARROW * rows, args.wq_any.shape[1], args.up_any.shape[1]
    rounds = args.orders.shape[0]
    chunks = rows // CHUNK
    depth = -(-(rounds * (length // GROUP) + args.docs.shape[0]) // LANES) * LANES
    weights = [(width, hidden), (hidden, width), (heads, width), (width, 2 * heads)]
    cut = [pieces(members, shape) for shape in weights]
    args = vars(args)
    in_specs = [IN_SMEM if k == DOCS else ANYWHERE if k.endswith(FROM_HBM) else IN_VMEM for k in args]
    outs = dict(
        out_one=((rows, width), HALF),
        out_two=((rows, width), HALF),
        grad_one=((rows, width), HALF),
        grad_two=((rows, width), HALF),
        small=((8, width), FLOAT),
    )
    out_shape = [jax.ShapeDtypeStruct(*o) for o in outs.values()] + [jax.ShapeDtypeStruct(shape, HALF) for shape in cut]
    out_specs = [ANYWHERE] * 4 + [IN_VMEM] + [ANYWHERE] * len(cut)
    tall = pltpu.VMEM((length, width), HALF)
    slim = pltpu.VMEM((length, heads), HALF)
    gather_sems, scatter_sems = DMA((4, 3 * chunks)), DMA((4, 3 * chunks))
    sum_sems = DMA((4, 2 * (members.bit_length() - 1)))
    ring_sems = DMA((2, 4 * (members - 1)))
    scratch = dict(
        whole_one=tall,
        whole_two=tall,
        cotans=tall,
        grad_rows=tall,
        active=pltpu.VMEM((length, hidden), HALF),
        grad_hidden=pltpu.VMEM((length, hidden), HALF),
        queries=slim,
        keys=slim,
        values=slim,
        merged=slim,
        grad_merged=slim,
        grad_both=pltpu.VMEM((length, 2 * heads), HALF),
        logs=pltpu.VMEM((8, length), FLOAT),
        query_features=pltpu.VMEM((depth, length), HALF),
        key_features=pltpu.VMEM((depth, length), HALF),
        wq=pltpu.VMEM((width, heads), HALF),
        wv=pltpu.VMEM((width, heads), HALF),
        wo=pltpu.VMEM((heads, width), HALF),
        up=pltpu.VMEM((width, hidden), HALF),
        down=pltpu.VMEM((hidden, width), HALF),
        middle=pltpu.VMEM((rows, width), FLOAT),
        first_rows=pltpu.VMEM((rows, width), HALF),
        bias=pltpu.VMEM((max(rounds, band_steps(length)), BLOCK, BLOCK), FLOAT),
        totals=pltpu.VMEM((3 * length, heads), FLOAT),
        sums=pltpu.VMEM((8, width), FLOAT),
        near_out=pltpu.VMEM((2, rows, width), HALF),
        near_in=pltpu.VMEM((2, rows, width), HALF),
        far_out=pltpu.VMEM((rows, width), HALF),
        far_in=pltpu.VMEM((rows, width), HALF),
        narrow_all=pltpu.VMEM((NARROW, 8, width), FLOAT),
        wide_all=pltpu.VMEM((members, 8, width), FLOAT),
        narrow_sent=DMA((NARROW,)),
        narrow_arrived=DMA((NARROW,)),
        wide_sent=DMA((members,)),
        wide_arrived=DMA((members,)),
        loads=DMA((8,)),
        stores=DMA((4,)),
        ready=pltpu.SemaphoreType.REGULAR,
        gather_sent=gather_sems,
        gather_arrived=gather_sems,
        scatter_sent=scatter_sems,
        scatter_arrived=scatter_sems,
        ring_sent=ring_sems,
        ring_arrived=ring_sems,
        ring_kept=DMA((2, 2 * members)),
        sum_sent=sum_sems,
        sum_arrived=sum_sems,
        sum_stored=DMA((4,)),
    )
    sum_buffers = [pltpu.VMEM(shape, HALF) for shape in cut]

    def kernel(*refs):
        count = len(args) + len(outs)
        named = dict(zip([*args, *outs], refs[:count]))
        results, rest = refs[count : count + len(cut)], refs[count + len(cut) :]
        named |= dict(zip(scratch, rest))
        rest = rest[len(scratch) :]
        ref = SimpleNamespace(**named, sum_results=results, sum_data=rest[: len(cut)], sum_landed=rest[len(cut) :])
        ref.grad_query = ref.grad_both.at[:, pl.ds(0, heads)]
        ref.grad_value = ref.grad_both.at[:, pl.ds(heads, heads)]
        layer(members, ref)

    found = pl.pallas_call(
        kernel,
        out_shape=out_shape,
        in_specs=in_specs,
        out_specs=out_specs,
        scratch_shapes=[*scratch.values(), *sum_buffers, *sum_buffers],
        compiler_params=pltpu.CompilerParams(collective_id=0, has_side_effects=True, vmem_limit_bytes=VMEM_LIMIT),
        name=layer.__name__,
    )(*args.values())
    sums = [result.reshape(shape) for result, shape in zip(found[len(outs) :], weights)]
    return SimpleNamespace(**dict(zip(outs, found))), sums


def finish(*refs):
    up, down, out, both, small, *rows = refs[:9]
    grad_up, grad_down, grad_out, grad_query, grad_value, *rest = refs[9:]
    heads = grad_query.shape[1]
    grad_up[...] = up[...].astype(FLOAT)
    grad_down[...] = down[...].astype(FLOAT)
    grad_out[...] = out[...].astype(FLOAT)
    grad_query[...] = both[:, :heads].astype(FLOAT)
    grad_value[...] = both[:, heads:].astype(FLOAT)
    for source, target in zip(rows, rest):
        target[...] = source[...]
    for source, target in zip((0, 1, 2, 3, 5, 6), rest[len(rows) :]):
        target[...] = small[source : source + 1, :]
    counts = rest[-1]
    for index in range(counts.shape[0]):
        counts[index : index + 1, :] = small[4:5, index * LANES : index * LANES + counts.shape[1]].astype(jnp.int32)


def run_finish(grads, small, rows, rounds):
    up, down, out, both = grads
    parts = 8
    vector = jax.ShapeDtypeStruct((1, small.shape[1]), FLOAT)
    taken = [up, down, out, both, small, *rows]
    given = [
        jax.ShapeDtypeStruct(up.shape, FLOAT),
        jax.ShapeDtypeStruct(down.shape, FLOAT),
        jax.ShapeDtypeStruct(out.shape, FLOAT),
        jax.ShapeDtypeStruct((both.shape[0], both.shape[1] // 2), FLOAT),
        jax.ShapeDtypeStruct((both.shape[0], both.shape[1] // 2), FLOAT),
        *[jax.ShapeDtypeStruct(r.shape, r.dtype) for r in rows],
        *[vector] * 6,
        jax.ShapeDtypeStruct((rounds, NB), jnp.int32),
    ]

    def spec(array):
        if array.shape[0] < LANES:
            return pl.BlockSpec(array.shape, lambda i: (0, 0))
        return pl.BlockSpec((array.shape[0] // parts, array.shape[1]), lambda i: (i, 0))

    return pl.pallas_call(
        finish,
        grid=(parts,),
        out_shape=given,
        in_specs=[spec(a) for a in taken],
        out_specs=[spec(a) for a in given],
        compiler_params=pltpu.CompilerParams(vmem_limit_bytes=VMEM_LIMIT),
        name=finish.__name__,
    )(*taken)


def per_device(
    stream_one,
    stream_two,
    attention_gain,
    attention_shift,
    query_proj,
    value_proj,
    output_proj,
    forward_gain,
    forward_shift,
    up_proj,
    up_bias,
    down_proj,
    down_bias,
    bucket_ids,
    sort_orders,
    doc_lengths,
    cotan_one,
    cotan_two,
):
    members = lax.axis_size("wide")
    row = lambda vector: vector.reshape(1, -1)
    found, grads = run_layer(
        members,
        SimpleNamespace(
            stream_one_any=stream_one,
            stream_two=stream_two,
            gain_one=row(attention_gain),
            shift_one=row(attention_shift),
            wq_any=query_proj,
            wv_any=value_proj,
            wo_any=output_proj,
            gain_two=row(forward_gain),
            shift_two=row(forward_shift),
            up_any=up_proj,
            up_bias=row(up_bias),
            down_any=down_proj,
            down_bias=row(down_bias),
            buckets=bucket_ids.T,
            orders=sort_orders[0],
            docs=doc_lengths[0],
            cotan_one_any=cotan_one,
            cotan_two_any=cotan_two,
        ),
    )
    rows = [found.out_one, found.out_two, found.grad_one, found.grad_two]
    grad_up, grad_down, grad_out, grad_query, grad_value, *rest = run_finish(
        grads, found.small, rows, sort_orders.shape[1]
    )
    gain_one, shift_one, gain_two, shift_two, bias_up, bias_down = [vector.reshape(-1) for vector in rest[4:10]]
    return (
        *rest[:4],
        gain_one,
        shift_one,
        grad_query,
        grad_value,
        grad_out,
        gain_two,
        shift_two,
        grad_up,
        bias_up,
        grad_down,
        bias_down,
        rest[10],
    )


def solution(mesh):
    rows = P(("wide", "narrow"), None)
    columns = P(None, "narrow")
    return jax.shard_map(
        per_device,
        mesh=mesh,
        in_specs=(
            rows,
            rows,
            P(),
            P(),
            columns,
            columns,
            P("narrow", None),
            P(),
            P(),
            columns,
            P("narrow"),
            P("narrow", None),
            P(),
            rows,
            P("wide", None, None),
            P("wide", None),
            rows,
            rows,
        ),
        out_specs=(
            rows,
            rows,
            rows,
            rows,
            P(),
            P(),
            columns,
            columns,
            P("narrow", None),
            P(),
            P(),
            columns,
            P("narrow"),
            P("narrow", None),
            P(),
            P(),
        ),
        check_vma=False,
    )
```

time: 1810 us -> 243 us (0.13)
  local copies, waits for them, and re-layouts: 780 us -> 0 us
  waiting for transfers between devices: 517 us -> 0 us
  matrix products: 295 us -> 0 us
  Pallas kernels: 0 us -> 242 us
  other arithmetic: 143 us -> 0 us
  blocking collectives: 59.9 us -> 0 us
    gather x16 -> x0, local copies, waits for them, and re-layouts: 621 us -> none  [the longest x11 463 us: pick_rows(): return jnp.take(matrix, indices, axis=0)]
    psum x1 -> x0, waiting for transfers between devices: 341 us -> none  [per_device(): lax.psum((grad_query_weights, grad_value_weights, grad_output, grad_up, g...]
    dot_general x21 -> x0, matrix products: 295 us -> none  [the longest x1 95 us: per_device(): jnp.einsum('rchij,rcihd->rcjhd', grad_scores, query_sorted, preferred_ele...]
    pallas_call x0 -> x2, Pallas kernels: none -> 242 us  [the longest x1 232 us: run_layer(): pl.pallas_call(kernel, out_shape=out_shape, in_specs=in_specs, out_specs=...]
    reduce_scatter x4 -> x0, waiting for transfers between devices: 99.2 us -> none  [the longest x1 61.1 us: per_device(): lax.psum_scatter(jnp.dot(merged, output_proj, preferred_element_type=FLOA...]
    reduce_sum x17 -> x0, other arithmetic: 86.7 us -> none  [the longest x2 36 us: restore(): jnp.sum(by_round(sorted_grad.reshape(round_count, length, head_count, HD)...]
    reshape x7 -> x0, local copies, waits for them, and re-layouts: 77.7 us -> none  [the longest x3 54.3 us: restore(): sorted_grad.reshape(round_count, length, head_count, HD)]
    all_gather x4 -> x0, waiting for transfers between devices: 75.8 us -> none  [the longest x1 27.7 us: per_device(): gathered_two = lax.all_gather(normed_two, 'narrow', axis=0, tiled=True)]
  transfers between devices with their start and end apart: 9 -> 0, of which waited for: 6 -> 0; matrix products, arithmetic and copies ran while one was open for 6% -> 0% of each run, Pallas kernels for 0% -> 0%
where the time goes in v3:
time: 243 us
  Pallas kernels  242 us (100%)
    pallas_call x1, Pallas kernels, run_layer(): pl.pallas_call(kernel, out_shape=out_shape, in_specs=in_specs, out_specs=...  232 us
    pallas_call x1, Pallas kernels, run_finish(): pl.pallas_call(finish, grid=(parts,), out_shape=given, in_specs=[spec(a)...  10.4 us

profile of v3, /device:TPU:0, one launch (start us, length us, event | category | flops | bytes accessed | tf_op | source)
XLA Modules:
  0.0 242.9 jit_solution(10652889659349919883)
XLA Ops:
  0.7 231.7 %layer.1 = (bf16[384,1024]{1,0:T(8,128)(2,1)}, bf16[384,1024]{1,0:T(8,128)(2,1)}, bf16[384,1024]{1,0:T(8,128)(2,1)}, bf16[384,1024]{1,0:T(8,128)(2,1)}, f32[8,10...) custom-call(bf16[384,1024]{1,0:T(8,128)(2,1)} %refs_0_.1, ...), custom_call_target="tpu_custom_call" | custom-call | tf_op jit(solution)/shard_map/layer/pallas_call | solution.py:1065
  232.4 10.4 %finish.1 = (f32[1024,1024]{1,0:T(8,128)}, f32[1024,1024]{1,0:T(8,128)}, f32[256,1024]{1,0:T(8,128)}, f32[1024,256]{1,0:T(8,128)}, f32[1024,256]{1,0:T(8,128)}, ...) custom-call(bf16[1024,1024]{1,0:T(8,128)(2,1)} %bitcast.19, ...), custom_call_target="tpu_custom_call" | custom-call | tf_op jit(solution)/shard_map/finish/pallas_call | solution.py:1117
